TPU v7x, 32 devices: a whole 2x2x4 slice. The times are simulated.
32 devices in a mesh: tm: 8 (over z, y), swath: 4 (over x, core).
Axes of the slice: x: 2, y: 2, z: 4, core: 2. Of those that a mesh axis runs over, the one named last changes fastest.
Arguments:
- design: bfloat16 [8, 2048, 512], P('tm', 'swath'), may hold values from -6 to 6
- process: bfloat16 [8, 512, 512], P('tm', 'swath')
- prior_prec: float32 [8, 512], P('tm', 'swath'), may hold values from 0.05 to 0.5
- routes: int32 [8, 16], P('tm', 'swath'), may hold values from -1 to 7, as said below
- counts: int32 [8, 4], P('tm', 'swath'), may hold values from 1 to 4
Outputs:
- reduced_diag: float32 [8, 512, 512], P('tm', 'swath')
- reduced_coupling: float32 [8, 512, 512], P('tm', 'swath')
Inputs may be any that keep to these rules, and one draw needn't show every extreme that they name: `routes`: each value is the holder's own time block i or i + 1, or -1 only where i + 1 would be 8; of one holder's 4 blocks, exactly 2 name i and the others i + 1 or -1.
All inputs are finite; a program needn't handle non-finite values.
Results may differ from a plain program's by a relative error of at most 0.00073.
Values may be sent and summed in bfloat16 or wider, within the bound.
A program may use at most 64 MiB of HBM per device.

v0:
```python
import functools

import jax
import jax.numpy as jnp
from jax import lax
from jax.experimental import pallas as pl
from jax.experimental.pallas import tpu as pltpu
from jax.sharding import PartitionSpec as P

LEVELS = 3
PIECES = 4


def split(x):
    high = x.astype(jnp.bfloat16)
    return high, (x - high.astype(jnp.float32)).astype(jnp.bfloat16)


def dot3(a, b, left):
    (ah, al), (bh, bl) = a, b
    dot = functools.partial(
        lax.dot_general,
        dimension_numbers=(((left,), (0,)), ((), ())),
        preferred_element_type=jnp.float32,
    )
    return dot(ah, bh) + (dot(ah, bl) + dot(al, bh))


def factor_inverse(m, width=8):
    n = m.shape[0]
    groups = n // width
    rows = [m[width * g : width * (g + 1), :] for g in range(groups)]
    lane = lax.broadcasted_iota(jnp.int32, (width, n), 1)
    sub = lax.broadcasted_iota(jnp.int32, (width, n), 0)
    spread = lambda x: jnp.broadcast_to(x, (width, n))
    for g in range(groups):
        first = width * g
        inside = (lane >= first) & (lane < first + width)
        columns = {
            h: [spread(rows[h][:, first + s : first + s + 1]) for s in range(width)]
            for h in range(g, groups)
        }
        entry = {
            (k, s): spread(columns[g][s][k : k + 1, :])
            for s in range(width)
            for k in range(s, width)
        }
        solved = [
            jnp.where(lane == first + s, 1.0, jnp.where(inside, 0.0, spread(rows[g][s : s + 1, :])))
            for s in range(width)
        ]
        scale, lower = [], {}
        for s in range(width):
            scale.append(lax.rsqrt(entry[s, s]))
            solved[s] = solved[s] * scale[s]
            for k in range(s + 1, width):
                lower[k, s] = entry[k, s] * scale[s]
            for k in range(s + 1, width):
                for t in range(s + 1, k + 1):
                    entry[k, t] = entry[k, t] - lower[k, s] * lower[t, s]
                solved[k] = solved[k] - lower[k, s] * solved[s]
        back = list(solved)
        for s in range(width - 1, -1, -1):
            back[s] = back[s] * scale[s]
            for k in range(s):
                back[k] = back[k] - lower[s, k] * back[s]
        for h in range(g + 1, groups):
            left = jnp.where(inside, 0.0, rows[h])
            for s in range(width - 1, -1, -1):
                left = left - columns[h][s] * back[s]
            rows[h] = left
        group = solved[0]
        for s in range(1, width):
            group = jnp.where(sub == s, solved[s], group)
        rows[g] = group
    out = jnp.concatenate(rows, axis=0)
    down = lax.broadcasted_iota(jnp.int32, (n, n), 0)
    across = lax.broadcasted_iota(jnp.int32, (n, n), 1)
    return jnp.where(down >= across, out, 0.0)


def factor_kernel(diag_ref, high, low, work, beside=None):
    blocks, rows, order = diag_ref.shape
    work[...] = diag_ref[...]
    for i in range(blocks):
        for k in range(i, blocks):
            here = work[i, :, k * rows : (k + 1) * rows]
            there = work[k, :, i * rows : (i + 1) * rows]
            work[i, :, k * rows : (k + 1) * rows] = 0.5 * (here + there.T)
    down = lax.broadcasted_iota(jnp.int32, (rows, rows), 0)
    across = lax.broadcasted_iota(jnp.int32, (rows, rows), 1)
    unit = jnp.where(down == across, 1.0, 0.0)
    column_block = lax.broadcasted_iota(jnp.int32, (rows, order), 1) // rows

    def step(j, carry):
        at = pl.ds(pl.multiple_of(j * rows, rows), rows)
        if beside is not None:
            beside(j)
        inverse = factor_inverse(work[j, :, at])
        work[j, :, at] = unit
        solved = dot3(split(inverse), split(work[j]), 1)
        solved_high, solved_low = split(solved)
        high[at, :] = solved_high
        low[at, :] = solved_low
        for i in range(1, blocks):

            @pl.when(i > j)
            def _():
                cut = slice(i * rows, (i + 1) * rows)
                left = (high[at, cut], low[at, cut])
                work[i, :, at] = jnp.zeros((rows, rows), jnp.float32)
                work[i] = work[i] - dot3(left, (solved_high, solved_low), 0)

        keep = column_block <= j
        high[at, :] = jnp.where(keep, solved_high, 0.0).astype(jnp.bfloat16)
        low[at, :] = jnp.where(keep, solved_low, 0.0).astype(jnp.bfloat16)
        return carry

    lax.fori_loop(0, blocks, step, 0)


def put_terms(index, inverse_high, inverse_low, parts_ref, out_ref, high, low):
    blocks, _, rows, order = parts_ref.shape
    for part in range(2):
        across = slice(part * order, (part + 1) * order)
        right = [split(parts_ref[i, part]) for i in range(blocks)]
        right = [jnp.concatenate([r[k] for r in right], axis=0) for k in range(2)]
        for j in range(blocks):
            at, deep = slice(j * rows, (j + 1) * rows), (j + 1) * rows
            left = (inverse_high[at, :deep], inverse_low[at, :deep])
            solved = dot3(left, (right[0][:deep], right[1][:deep]), 1)
            solved_high, solved_low = split(solved)
            high[at, across] = solved_high
            low[at, across] = solved_low
    mine = index * rows
    for k, (first, second) in enumerate(((0, 0), (0, 1), (1, 1), (1, 0))):
        cut = pl.ds(pl.multiple_of(first * order + mine, rows), rows)
        across = slice(second * order, (second + 1) * order)
        out_ref[k] = dot3((high[:, cut], low[:, cut]), (high[:, across], low[:, across]), 0)


MESH = pl.DeviceIdType.MESH


def across(place, bit):
    return place + bit - 2 * bit * ((place // bit) % 2)


class Spread:
    def __init__(self, size, place, block, send_sem, recv_sem, own=None, cut=None, base=0):
        bits = [size >> (k + 1) for k in range(size.bit_length() - 1)]
        self.plan = [(b, 0) for b in bits]
        for k, b in enumerate(bits):
            earlier = [0]
            for e in bits[:k]:
                earlier += [m + e for m in earlier]
            self.plan += [(b, m) for m in earlier if m]
        self.copies, self.arrived = [], set()
        part = lambda held: block.at[held] if cut is None else block.at[held, cut]
        for k, (b, m) in enumerate(self.plan):
            held = place
            for e in bits:
                if m & e:
                    held = across(held, e)
            self.copies.append(
                pltpu.make_async_remote_copy(
                    src_ref=own if own is not None and m == 0 else part(held),
                    dst_ref=part(held),
                    send_sem=send_sem.at[base + k],
                    recv_sem=recv_sem.at[base + k],
                    device_id={"swath": across(place, b)},
                    device_id_type=MESH,
                )
            )

    def start_own(self):
        for copy, (b, m) in zip(self.copies, self.plan):
            if m == 0:
                copy.start()

    def forward(self):
        for copy, (b, m) in zip(self.copies, self.plan):
            if m:
                last = m & -m
                source = self.plan.index((last, m - last))
                if source not in self.arrived:
                    self.copies[source].wait_recv()
                    self.arrived.add(source)
                copy.start()

    def finish(self):
        for k, copy in enumerate(self.copies):
            if k not in self.arrived:
                copy.wait_recv()
        for copy in self.copies:
            copy.wait_send()


def greet(distance, times, size, spread_too):
    place, me = lax.axis_index("swath"), lax.axis_index("tm")
    barrier = pltpu.get_barrier_semaphore()
    behind, ahead = me >= distance, me + distance < times

    @pl.when(behind)
    def _():
        pl.semaphore_signal(barrier, inc=1, device_id={"tm": me - distance}, device_id_type=MESH)

    @pl.when(ahead)
    def _():
        pl.semaphore_signal(barrier, inc=1, device_id={"tm": me + distance}, device_id_type=MESH)

    count = behind.astype(jnp.int32) + ahead.astype(jnp.int32)
    if spread_too:
        bits = [size >> (k + 1) for k in range(size.bit_length() - 1)]
        for b in bits:
            pl.semaphore_signal(
                barrier, inc=1, device_id={"swath": across(place, b)}, device_id_type=MESH
            )
        count = count + len(bits)
    pl.semaphore_wait(barrier, count)
    return place, me, behind, ahead


def handed(me, distance, behind, ahead, moves, send_sem, recv_sem):
    plan = []
    for k, (source, target, up) in enumerate(moves):
        copy = pltpu.make_async_remote_copy(
            src_ref=source,
            dst_ref=target,
            send_sem=send_sem.at[k],
            recv_sem=recv_sem.at[k],
            device_id={"tm": me + distance if up else me - distance},
            device_id_type=MESH,
        )
        plan.append((copy, target, ahead if up else behind, behind if up else ahead))

    def start(items):
        for copy, target, sends, receives in items:
            pl.when(sends)(copy.start)

    def receive(items):
        for copy, target, sends, receives in items:
            pl.when(receives)(copy.wait_recv)

            @pl.when(jnp.logical_not(receives))
            def _():
                target[...] = jnp.zeros(target.shape, target.dtype)

    def sent(items):
        for copy, target, sends, receives in items:
            pl.when(sends)(copy.wait_send)

    return plan, start, receive, sent


def step_kernel(distance, times, size, terms_ref, diag_ref, out_ref, out_diag_ref, land, diag_full,
                parts, high, low, work, solved_high, solved_low, move_send, move_recv,
                diag_send, diag_recv, part_send, part_recv):
    place, me, behind, ahead = greet(distance, times, size, True)
    piece = diag_ref.shape[0] // PIECES
    cuts = [pl.ds(c * piece, piece) for c in range(PIECES)]
    moves = []
    for cut in cuts:
        moves.append((terms_ref.at[0, cut], land.at[0, cut], True))
        moves.append((terms_ref.at[2, cut], land.at[1, cut], False))
    moves.append((terms_ref.at[3], parts.at[place, 0], False))
    moves.append((terms_ref.at[1], parts.at[place, 1], True))
    plan, start, receive, sent = handed(
        me, distance, behind, ahead, moves, move_send, move_recv
    )
    coupled = 2 * PIECES
    start(plan[:coupled])
    spreads = []
    for c, cut in enumerate(cuts):
        receive(plan[2 * c : 2 * c + 2])
        if c == PIECES - 1:
            start(plan[coupled:])
        mine = diag_ref[cut] - land[0, cut] - land[1, cut]
        out_diag_ref[cut] = mine
        diag_full[place, cut] = mine
        spreads.append(
            Spread(size, place, diag_full, diag_send, diag_recv, None, cut, c * (size - 1))
        )
        spreads[c].start_own()
    for spread in spreads:
        spread.forward()
    for spread in spreads:
        spread.finish()
    part_spread = Spread(size, place, parts, part_send, part_recv)
    blocks = diag_full.shape[0]

    def beside(j):
        @pl.when(j == 1)
        def _():
            receive(plan[coupled:])
            part_spread.start_own()

        @pl.when(j == blocks - 1)
        def _():
            part_spread.forward()

    factor_kernel(diag_full, high, low, work, beside)
    part_spread.finish()
    sent(plan)
    put_terms(place, high, low, parts, out_ref, solved_high, solved_low)


def step(distance, terms_in, diag_rows):
    times, size = lax.axis_size("tm"), lax.axis_size("swath")
    rows, order = diag_rows.shape
    vmem = pl.BlockSpec(memory_space=pltpu.VMEM)
    dma = pltpu.SemaphoreType.DMA
    return pl.pallas_call(
        functools.partial(step_kernel, distance, times, size),
        out_shape=(
            jax.ShapeDtypeStruct((4, rows, order), jnp.float32),
            jax.ShapeDtypeStruct((rows, order), jnp.float32),
        ),
        in_specs=[vmem] * 2,
        out_specs=(vmem,) * 2,
        scratch_shapes=[
            pltpu.VMEM((2, rows, order), jnp.float32),
            pltpu.VMEM((size, rows, order), jnp.float32),
            pltpu.VMEM((size, 2, rows, order), jnp.float32),
            pltpu.VMEM((order, order), jnp.bfloat16),
            pltpu.VMEM((order, order), jnp.bfloat16),
            pltpu.VMEM((size, rows, order), jnp.float32),
            pltpu.VMEM((order, 2 * order), jnp.bfloat16),
            pltpu.VMEM((order, 2 * order), jnp.bfloat16),
            dma((2 * PIECES + 2,)),
            dma((2 * PIECES + 2,)),
            dma((PIECES * (size - 1),)),
            dma((PIECES * (size - 1),)),
            dma((size - 1,)),
            dma((size - 1,)),
        ],
        compiler_params=pltpu.CompilerParams(collective_id=distance, has_side_effects=True),
    )(terms_in, diag_rows)


def last_kernel(distance, times, size, terms_ref, diag_ref, out_diag_ref, out_coup_ref, land, move_send, move_recv):
    place, me, behind, ahead = greet(distance, times, size, False)
    moves = [
        (terms_ref.at[3], land.at[2], False),
        (terms_ref.at[0], land.at[0], True),
        (terms_ref.at[2], land.at[1], False),
    ]
    plan, start, receive, sent = handed(
        me, distance, behind, ahead, moves, move_send, move_recv
    )
    start(plan)
    receive(plan)
    out_coup_ref[...] = -land[2]
    out_diag_ref[...] = diag_ref[...] - land[0] - land[1]
    sent(plan)


def last(distance, terms_in, diag_rows):
    times, size = lax.axis_size("tm"), lax.axis_size("swath")
    rows, order = diag_rows.shape
    vmem = pl.BlockSpec(memory_space=pltpu.VMEM)
    return pl.pallas_call(
        functools.partial(last_kernel, distance, times, size),
        out_shape=(jax.ShapeDtypeStruct((rows, order), jnp.float32),) * 2,
        in_specs=[vmem] * 2,
        out_specs=(vmem,) * 2,
        scratch_shapes=[
            pltpu.VMEM((3, rows, order), jnp.float32),
            pltpu.SemaphoreType.DMA((3,)),
            pltpu.SemaphoreType.DMA((3,)),
        ],
        compiler_params=pltpu.CompilerParams(collective_id=distance, has_side_effects=True),
    )(terms_in, diag_rows)


def weigh_kernel(total_slots, block_rows, design_ref, process_ref, routes_ref, counts_ref, near_ref, sent_ref):
    me = lax.axis_index("tm")
    block_count = routes_ref.shape[1]
    slot_count = block_count // 2
    weighted = []
    for r in range(block_count):
        raw = design_ref[r * block_rows : (r + 1) * block_rows, :].astype(jnp.float32)
        mean_sq = jnp.mean(raw * raw, axis=-1, keepdims=True)
        weighted.append((raw * lax.rsqrt(4.0 * total_slots * (mean_sq + 1e-06))).astype(jnp.bfloat16))
    for out_ref, owner in ((near_ref, me), (sent_ref, me + 1)):
        place = jnp.int32(0)
        chosen = [jnp.full((), -1, jnp.int32) for _ in range(slot_count)]
        for r in range(block_count):
            named = routes_ref[0, r] == owner
            live = r < counts_ref[0, 0]
            for k in range(slot_count):
                chosen[k] = jnp.where(named & live & (place == k), r, chosen[k])
            place = place + named.astype(jnp.int32)
        for k in range(slot_count):
            block = jnp.zeros(weighted[0].shape, jnp.float32)
            for r in range(block_count):
                block = jnp.where(chosen[k] == r, weighted[r].astype(jnp.float32), block)
            out_ref[k * block_rows : (k + 1) * block_rows, :] = block.astype(jnp.bfloat16)
        out_ref[slot_count * block_rows :, :] = process_ref[...]


def weigh(design, process, routes, counts, total_slots):
    order = process.shape[1]
    block_count = routes.shape[1]
    block_rows = design.shape[0] // block_count
    rows = block_count // 2 * block_rows + process.shape[0]
    vmem, smem = (pl.BlockSpec(memory_space=m) for m in (pltpu.VMEM, pltpu.SMEM))
    return pl.pallas_call(
        functools.partial(weigh_kernel, total_slots, block_rows),
        out_shape=(jax.ShapeDtypeStruct((rows, order), jnp.bfloat16),) * 2,
        in_specs=[vmem, vmem, smem, smem],
        out_specs=(vmem,) * 2,
    )(design, process, routes, counts)


def first_kernel(times, size, near_ref, sent_ref, prior_ref, out_ref, out_diag_ref, near, far, prior,
                 diag_full, parts, high, low, work, solved_high, solved_low, move_send, move_recv,
                 near_send, near_recv, prior_send, prior_recv, far_send, far_recv):
    place, me, behind, ahead = greet(1, times, size, True)
    rows, order = diag_full.shape[1:]
    observed = near.shape[1] - rows
    piece = near.shape[1] // PIECES
    cuts = [pl.ds(c * piece, piece) for c in range(PIECES)]
    moves = [(sent_ref.at[cut], far.at[place, cut], True) for cut in cuts]
    plan, start, receive, sent = handed(me, 1, behind, ahead, moves, move_send, move_recv)
    start(plan)
    near_spread = Spread(size, place, near, near_send, near_recv, near_ref)
    prior_spread = Spread(size, place, prior, prior_send, prior_recv, prior_ref)
    near_spread.start_own()
    prior_spread.start_own()
    near[place] = near_ref[...]
    prior[place] = prior_ref[...]
    far_spreads = []
    for c, cut in enumerate(cuts):
        receive(plan[c : c + 1])
        far_spreads.append(
            Spread(size, place, far, far_send, far_recv, None, cut, c * (size - 1))
        )
        far_spreads[c].start_own()
    near_spread.forward()
    prior_spread.forward()
    near_spread.finish()
    prior_spread.finish()
    for spread in far_spreads:
        spread.forward()
    square = (rows, rows)
    unit = lax.broadcasted_iota(jnp.int32, square, 0) == lax.broadcasted_iota(jnp.int32, square, 1)

    def add_grams(source):
        for b in range(size):
            cut = slice(b * rows, (b + 1) * rows)
            total = source[b, observed:].astype(jnp.float32)
            for i in range(size):
                total = total + lax.dot_general(
                    source[i, :observed, cut],
                    source[i, :observed, :],
                    (((0,), (0,)), ((), ())),
                    preferred_element_type=jnp.float32,
                )
            yield b, cut, total

    for b, cut, total in add_grams(near):
        diag_full[b] = total
        diag_full[b, :, cut] += jnp.where(unit, jnp.broadcast_to(prior[b][:1], square), 0.0)
        parts[b, 0] = near[b, observed:].astype(jnp.float32)
    for spread in far_spreads:
        spread.finish()
    for b, cut, total in add_grams(far):
        diag_full[b] += total
        for q in range(size):
            turned = far[q, observed:, cut].astype(jnp.float32).T
            parts[b, 1, :, q * rows : (q + 1) * rows] = turned
    out_diag_ref[...] = diag_full[place]
    factor_kernel(diag_full, high, low, work)
    sent(plan)
    put_terms(place, high, low, parts, out_ref, solved_high, solved_low)


def first(near, sent, prior):
    times, size = lax.axis_size("tm"), lax.axis_size("swath")
    order = near.shape[1]
    rows = order // size
    vmem = pl.BlockSpec(memory_space=pltpu.VMEM)
    dma = pltpu.SemaphoreType.DMA
    return pl.pallas_call(
        functools.partial(first_kernel, times, size),
        out_shape=(
            jax.ShapeDtypeStruct((4, rows, order), jnp.float32),
            jax.ShapeDtypeStruct((rows, order), jnp.float32),
        ),
        in_specs=[vmem] * 3,
        out_specs=(vmem,) * 2,
        scratch_shapes=[
            pltpu.VMEM((size,) + near.shape, jnp.bfloat16),
            pltpu.VMEM((size,) + near.shape, jnp.bfloat16),
            pltpu.VMEM((size,) + prior.shape, jnp.float32),
            pltpu.VMEM((size, rows, order), jnp.float32),
            pltpu.VMEM((size, 2, rows, order), jnp.float32),
            pltpu.VMEM((order, order), jnp.bfloat16),
            pltpu.VMEM((order, order), jnp.bfloat16),
            pltpu.VMEM((size, rows, order), jnp.float32),
            pltpu.VMEM((order, 2 * order), jnp.bfloat16),
            pltpu.VMEM((order, 2 * order), jnp.bfloat16),
            dma((PIECES,)),
            dma((PIECES,)),
        ]
        + [dma((size - 1,))] * 4
        + [dma((PIECES * (size - 1),))] * 2,
        compiler_params=pltpu.CompilerParams(collective_id=0, has_side_effects=True),
    )(near, sent, prior)


def shards(design, process, prior_prec, routes, counts):
    row_count = process.shape[1]
    block_count = routes.shape[1]
    block_rows = design.shape[1] // block_count
    total_slots = 2 * (block_count // 2) * block_rows * lax.axis_size("swath")
    near, sent = weigh(design[0], process[0], routes, counts, total_slots)
    prior = jnp.broadcast_to(prior_prec, (8, row_count))
    out, diag_rows = first(near, sent, prior)
    for level in range(1, LEVELS):
        out, diag_rows = step(2 ** (level - 1), out, diag_rows)
    diag_rows, coup_rows = last(2 ** (LEVELS - 1), out, diag_rows)
    return (diag_rows[None], coup_rows[None])


def solution(mesh):
    return jax.shard_map(
        shards,
        mesh=mesh,
        in_specs=(
            P("tm", "swath", None),
            P("tm", "swath", None),
            P("tm", "swath"),
            P("tm", "swath"),
            P("tm", "swath"),
        ),
        out_specs=(P("tm", "swath", None), P("tm", "swath", None)),
        check_vma=False,
    )
```

profile of v0, /device:TPU:0, one launch (start us, length us, event | category | flops | bytes accessed | tf_op | source)
XLA Modules:
  0.0 178.0 jit_solution(9945644783844723789)
XLA Ops:
  1.3 0.0 copy-start.1
  1.3 0.6 copy-done.1
  1.9 0.6 broadcast_in_dim.14.prior_ref
  2.5 2.3 %shard_map.68 = (bf16[384,512]{1,0:T(8,128)(2,1)}, bf16[384,512]{1,0:T(8,128)(2,1)}) custom-call(bf16[512,512]{1,0:T(8,128)(2,1)} %bitcast.5, bf16[128,512]{1,0:T(8,128)(2,1)} %bitcast.8, s32[1,4]{1,0:T(1,128)} %routes_ref.1, s32[1,1]{1,0:T(1,128)S(6)} %copy.9.counts_ref), custom_call_target="tpu_custom_call" | custom-call | tf_op jit(solution)/shard_map/pallas_call | solution.py:408
  4.9 50.1 %shard_map.69 = (f32[4,128,512]{2,1,0:T(8,128)}, f32[128,512]{1,0:T(8,128)}) custom-call(bf16[384,512]{1,0:T(8,128)(2,1)} %get-tuple-element.12.near_ref, bf16[384,512]{1,0:T(8,128)(2,1)} %get-tuple-element.13.sent_ref, f32[8,128]{1,0:T(8,128)} %broadcast_in_dim.14.prior_ref), custom_call_target="tpu_custom_call" | custom-call | tf_op jit(solution)/shard_map/pallas_call | solution.py:485
  55.0 43.6 %shard_map.70 = (f32[4,128,512]{2,1,0:T(8,128)}, f32[128,512]{1,0:T(8,128)}) custom-call(f32[4,128,512]{2,1,0:T(8,128)} %get-tuple-element.14.terms_ref, f32[128,512]{1,0:T(8,128)} %get-tuple-element.15.diag_ref), custom_call_target="tpu_custom_call" | custom-call | tf_op jit(solution)/shard_map/pallas_call | solution.py:313
  98.7 49.0 %shard_map.71 = (f32[4,128,512]{2,1,0:T(8,128)}, f32[128,512]{1,0:T(8,128)}) custom-call(f32[4,128,512]{2,1,0:T(8,128)} %get-tuple-element.16.terms_ref, f32[128,512]{1,0:T(8,128)} %get-tuple-element.17.diag_ref), custom_call_target="tpu_custom_call" | custom-call | tf_op jit(solution)/shard_map/pallas_call | solution.py:313
  147.7 27.9 %shard_map.72 = (f32[128,512]{1,0:T(8,128)}, f32[128,512]{1,0:T(8,128)}) custom-call(f32[4,128,512]{2,1,0:T(8,128)} %get-tuple-element.18.terms_ref, f32[128,512]{1,0:T(8,128)} %get-tuple-element.19.diag_ref), custom_call_target="tpu_custom_call" | custom-call | tf_op jit(solution)/shard_map/pallas_call | solution.py:362
  175.6 0.0 copy-start
  175.6 1.7 copy.10
  177.3 0.0 copy-done
  177.3 0.7 copy.11
Async XLA Ops:
  1.3 0.7 copy-start.1
  175.6 1.7 copy-start
where the time goes:
time: 178 us
  Pallas kernels  173 us (97%)
  local copies, waits for them, and re-layouts  3.66 us (2%)
    pallas_call x2, Pallas kernels, step(): pl.pallas_call(functools.partial(step_kernel, distance, times, size), out...  92.6 us
    pallas_call x1, Pallas kernels, first(): pl.pallas_call(functools.partial(first_kernel, times, size), out_shape=(j...  50.1 us
    pallas_call x1, Pallas kernels, last(): pl.pallas_call(functools.partial(last_kernel, distance, times, size), out...  27.9 us

commit v1 on v0

--- a/solution.py
+++ b/solution.py
@@ -9,6 +9,7 @@
 
 LEVELS = 3
 PIECES = 4
+W = 8
 
 
 def split(x):
@@ -26,53 +27,105 @@
     return dot(ah, bh) + (dot(ah, bl) + dot(al, bh))
 
 
-def factor_inverse(m, width=8):
+def joined(a, b, dims):
+    (ah, al), (bh, bl) = a, b
+    return lax.dot_general(
+        jnp.concatenate([ah, ah, al], axis=dims[0]),
+        jnp.concatenate([bh, bl, bh], axis=dims[1]),
+        (((dims[0],), (dims[1],)), ((), ())),
+        preferred_element_type=jnp.float32,
+    )
+
+def pivots(columns):
+    spread = lambda x: jnp.broadcast_to(x, columns[0].shape)
+    entry = {(k, s): spread(columns[s][k : k + 1, :]) for s in range(W) for k in range(s, W)}
+    scale, lower = [], {}
+    for s in range(W):
+        pivot = entry[s, s]
+        turned = 1.0 / pivot
+        scale.append(lax.rsqrt(pivot))
+        if s + 1 < W:
+            near = entry[s + 1, s]
+            entry[s + 1, s + 1] = entry[s + 1, s + 1] - (near * near) * turned
+        for k in range(s + 1, W):
+            lower[k, s] = entry[k, s] * scale[s]
+        for k in range(s + 2, W):
+            part = entry[k, s] * turned
+            for t in range(s + 1, k + 1):
+                entry[k, t] = entry[k, t] - part * entry[t, s]
+    return scale, lower
+
+def forward(values, scale, lower):
+    out = []
+    values = list(values)
+    for s in range(W):
+        out.append(values[s] * scale[s])
+        for k in range(s + 1, W):
+            values[k] = values[k] - lower[k, s] * out[s]
+    return out
+
+def factor_inverse(m, panel=32):
     n = m.shape[0]
-    groups = n // width
-    rows = [m[width * g : width * (g + 1), :] for g in range(groups)]
-    lane = lax.broadcasted_iota(jnp.int32, (width, n), 1)
-    sub = lax.broadcasted_iota(jnp.int32, (width, n), 0)
-    spread = lambda x: jnp.broadcast_to(x, (width, n))
-    for g in range(groups):
-        first = width * g
-        inside = (lane >= first) & (lane < first + width)
-        columns = {
-            h: [spread(rows[h][:, first + s : first + s + 1]) for s in range(width)]
-            for h in range(g, groups)
-        }
-        entry = {
-            (k, s): spread(columns[g][s][k : k + 1, :])
-            for s in range(width)
-            for k in range(s, width)
-        }
-        solved = [
-            jnp.where(lane == first + s, 1.0, jnp.where(inside, 0.0, spread(rows[g][s : s + 1, :])))
-            for s in range(width)
-        ]
-        scale, lower = [], {}
-        for s in range(width):
-            scale.append(lax.rsqrt(entry[s, s]))
-            solved[s] = solved[s] * scale[s]
-            for k in range(s + 1, width):
-                lower[k, s] = entry[k, s] * scale[s]
-            for k in range(s + 1, width):
-                for t in range(s + 1, k + 1):
-                    entry[k, t] = entry[k, t] - lower[k, s] * lower[t, s]
-                solved[k] = solved[k] - lower[k, s] * solved[s]
-        back = list(solved)
-        for s in range(width - 1, -1, -1):
-            back[s] = back[s] * scale[s]
-            for k in range(s):
-                back[k] = back[k] - lower[s, k] * back[s]
-        for h in range(g + 1, groups):
-            left = jnp.where(inside, 0.0, rows[h])
-            for s in range(width - 1, -1, -1):
-                left = left - columns[h][s] * back[s]
-            rows[h] = left
+    rows = [m[W * g : W * (g + 1), :] for g in range(n // W)]
+    lane = lax.broadcasted_iota(jnp.int32, (W, n), 1)
+    sub = lax.broadcasted_iota(jnp.int32, (W, n), 0)
+    spread = lambda x: jnp.broadcast_to(x, (W, n))
+    cleared = lambda x, first: jnp.where((lane >= first) & (lane < first + W), 0.0, x)
+    column = lambda h, first: [spread(rows[h][:, first + s : first + s + 1]) for s in range(W)]
+
+    def solve_rows(row, first, scale, lower):
+        row = cleared(row, first)
+        start = [jnp.where(lane == first + s, 1.0, spread(row[s : s + 1, :])) for s in range(W)]
+        solved = forward(start, scale, lower)
         group = solved[0]
-        for s in range(1, width):
+        for s in range(1, W):
             group = jnp.where(sub == s, solved[s], group)
-        rows[g] = group
+        return solved, group
+
+    def take(row, factors, solved, first):
+        row = cleared(row, first)
+        for s in range(W):
+            row = row - factors[s] * solved[s]
+        return row
+
+    per = panel // W
+    for p in range(n // panel):
+        end = (p + 1) * per
+        for q in range(0, per, 2):
+            g, h = p * per + q, p * per + q + 1
+            first, second = g * W, h * W
+            scale, lower = pivots(column(g, first))
+            cross = forward(column(h, first), scale, lower)
+            crossed = {(k, s): spread(cross[s][k : k + 1, :]) for s in range(W) for k in range(W)}
+            corner = column(h, second)
+            for t in range(W):
+                for s in range(W):
+                    corner[t] = corner[t] - cross[s] * crossed[t, s]
+            scale2, lower2 = pivots(corner)
+            others = range(h + 1, end)
+            left = {i: column(i, first) for i in others}
+            right = {i: column(i, second) for i in others}
+            solved, group = solve_rows(rows[g], first, scale, lower)
+            rows[g] = group
+            solved2, group2 = solve_rows(take(rows[h], cross, solved, first), second, scale2, lower2)
+            rows[h] = group2
+            for i in others:
+                one = forward(left[i], scale, lower)
+                two = right[i]
+                for t in range(W):
+                    for s in range(W):
+                        two[t] = two[t] - one[s] * crossed[t, s]
+                two = forward(two, scale2, lower2)
+                rows[i] = take(take(rows[i], one, solved, first), two, solved2, second)
+        if end < n // W:
+            edge = end * W
+            kept = lambda g: jnp.where((lane < (g + 1) * W) | (lane >= edge), rows[g], 0.0)
+            done = jnp.concatenate([kept(g) for g in range(p * per, end)], axis=0)
+            pair = split(done)
+            term = joined(pair, pair, (0, 0))
+            outside = (lane < p * panel) | (lane >= (p + 1) * panel)
+            for i in range(end, n // W):
+                rows[i] = jnp.where(outside, rows[i], 0.0) - term[W * i : W * (i + 1), :]
     out = jnp.concatenate(rows, axis=0)
     down = lax.broadcasted_iota(jnp.int32, (n, n), 0)
     across = lax.broadcasted_iota(jnp.int32, (n, n), 1)

time: 178 us -> 166 us (0.933)
  Pallas kernels: 173 us -> 161 us
    pallas_call x1, Pallas kernels: 50.1 us -> 43.4 us  [first(): pl.pallas_call(functools.partial(first_kernel, times, size), out_shape=(j...]
    pallas_call x2, Pallas kernels: 92.6 us -> 87.6 us  [step(): pl.pallas_call(functools.partial(step_kernel, distance, times, size), out...]
where the time goes in v1:
time: 166 us
  Pallas kernels  161 us (97%)
  local copies, waits for them, and re-layouts  3.66 us (2%)
    pallas_call x2, Pallas kernels, step(): pl.pallas_call(functools.partial(step_kernel, distance, times, size), out...  87.6 us
    pallas_call x1, Pallas kernels, first(): pl.pallas_call(functools.partial(first_kernel, times, size), out_shape=(j...  43.4 us
    pallas_call x1, Pallas kernels, last(): pl.pallas_call(functools.partial(last_kernel, distance, times, size), out...  27.9 us

profile of v1, /device:TPU:0, one launch (start us, length us, event | category | flops | bytes accessed | tf_op | source)
XLA Modules:
  0.0 166.2 jit_solution(4944912353833225459)
XLA Ops:
  1.3 0.0 copy-start.1
  1.3 0.6 copy-done.1
  1.9 0.6 broadcast_in_dim.14.prior_ref
  2.5 2.3 %shard_map.68 = (bf16[384,512]{1,0:T(8,128)(2,1)}, bf16[384,512]{1,0:T(8,128)(2,1)}) custom-call(bf16[512,512]{1,0:T(8,128)(2,1)} %bitcast.5, bf16[128,512]{1,0:T(8,128)(2,1)} %bitcast.8, s32[1,4]{1,0:T(1,128)} %routes_ref.1, s32[1,1]{1,0:T(1,128)S(6)} %copy.9.counts_ref), custom_call_target="tpu_custom_call" | custom-call | tf_op jit(solution)/shard_map/pallas_call | solution.py:461
  4.9 43.4 %shard_map.69 = (f32[4,128,512]{2,1,0:T(8,128)}, f32[128,512]{1,0:T(8,128)}) custom-call(bf16[384,512]{1,0:T(8,128)(2,1)} %get-tuple-element.12.near_ref, bf16[384,512]{1,0:T(8,128)(2,1)} %get-tuple-element.13.sent_ref, f32[8,128]{1,0:T(8,128)} %broadcast_in_dim.14.prior_ref), custom_call_target="tpu_custom_call" | custom-call | tf_op jit(solution)/shard_map/pallas_call | solution.py:538
  48.3 41.0 %shard_map.70 = (f32[4,128,512]{2,1,0:T(8,128)}, f32[128,512]{1,0:T(8,128)}) custom-call(f32[4,128,512]{2,1,0:T(8,128)} %get-tuple-element.14.terms_ref, f32[128,512]{1,0:T(8,128)} %get-tuple-element.15.diag_ref), custom_call_target="tpu_custom_call" | custom-call | tf_op jit(solution)/shard_map/pallas_call | solution.py:366
  89.3 46.5 %shard_map.71 = (f32[4,128,512]{2,1,0:T(8,128)}, f32[128,512]{1,0:T(8,128)}) custom-call(f32[4,128,512]{2,1,0:T(8,128)} %get-tuple-element.16.terms_ref, f32[128,512]{1,0:T(8,128)} %get-tuple-element.17.diag_ref), custom_call_target="tpu_custom_call" | custom-call | tf_op jit(solution)/shard_map/pallas_call | solution.py:366
  135.9 27.9 %shard_map.72 = (f32[128,512]{1,0:T(8,128)}, f32[128,512]{1,0:T(8,128)}) custom-call(f32[4,128,512]{2,1,0:T(8,128)} %get-tuple-element.18.terms_ref, f32[128,512]{1,0:T(8,128)} %get-tuple-element.19.diag_ref), custom_call_target="tpu_custom_call" | custom-call | tf_op jit(solution)/shard_map/pallas_call | solution.py:415
  163.8 0.0 copy-start
  163.8 1.7 %copy.10 = f32[1,128,512]{2,1,0:T(8,128)} copy(f32[1,128,512]{2,1,0:T(8,128)} %bitcast.7) | data formatting | bytes 524288
  165.5 0.0 copy-done
  165.5 0.7 copy.11
Async XLA Ops:
  1.3 0.7 copy-start.1
  163.8 1.7 %copy-start = (f32[128,512]{1,0:T(8,128)S(1)}, f32[128,512]{1,0:T(8,128)}, u32[]{:S(2)}) copy-start(f32[128,512]{1,0:T(8,128)} %get-tuple-element.21) | copy-start | bytes 786436

commit v2 on v1

v2 whole, which is shorter than its diff:
```python
import functools

import jax
import jax.numpy as jnp
from jax import lax
from jax.experimental import pallas as pl
from jax.experimental.pallas import tpu as pltpu
from jax.sharding import PartitionSpec as P

LEVELS = 3
W = 8
MESH = pl.DeviceIdType.MESH


def split(x):
    high = x.astype(jnp.bfloat16)
    return high, (x - high.astype(jnp.float32)).astype(jnp.bfloat16)

def joined(a, b, dims):
    (ah, al), (bh, bl) = a, b
    return lax.dot_general(
        jnp.concatenate([ah, ah, al], axis=dims[0]),
        jnp.concatenate([bh, bl, bh], axis=dims[1]),
        (((dims[0],), (dims[1],)), ((), ())),
        preferred_element_type=jnp.float32,
    )

def pivots(columns):
    spread = lambda x: jnp.broadcast_to(x, columns[0].shape)
    entry = {(k, s): spread(columns[s][k : k + 1, :]) for s in range(W) for k in range(s, W)}
    scale, lower = [], {}
    for s in range(W):
        pivot = entry[s, s]
        turned = 1.0 / pivot
        scale.append(lax.rsqrt(pivot))
        if s + 1 < W:
            near = entry[s + 1, s]
            entry[s + 1, s + 1] = entry[s + 1, s + 1] - (near * near) * turned
        for k in range(s + 1, W):
            lower[k, s] = entry[k, s] * scale[s]
        for k in range(s + 2, W):
            part = entry[k, s] * turned
            for t in range(s + 1, k + 1):
                entry[k, t] = entry[k, t] - part * entry[t, s]
    return scale, lower

def forward(values, scale, lower):
    out = []
    values = list(values)
    for s in range(W):
        out.append(values[s] * scale[s])
        for k in range(s + 1, W):
            values[k] = values[k] - lower[k, s] * out[s]
    return out

def factor_inverse(m, panel=32):
    n = m.shape[0]
    rows = [m[W * g : W * (g + 1), :] for g in range(n // W)]
    lane = lax.broadcasted_iota(jnp.int32, (W, n), 1)
    sub = lax.broadcasted_iota(jnp.int32, (W, n), 0)
    spread = lambda x: jnp.broadcast_to(x, (W, n))
    cleared = lambda x, first: jnp.where((lane >= first) & (lane < first + W), 0.0, x)
    column = lambda h, first: [spread(rows[h][:, first + s : first + s + 1]) for s in range(W)]

    def solve_rows(row, first, scale, lower):
        row = cleared(row, first)
        start = [jnp.where(lane == first + s, 1.0, spread(row[s : s + 1, :])) for s in range(W)]
        solved = forward(start, scale, lower)
        group = solved[0]
        for s in range(1, W):
            group = jnp.where(sub == s, solved[s], group)
        return solved, group

    def take(row, factors, solved, first):
        row = cleared(row, first)
        for s in range(W):
            row = row - factors[s] * solved[s]
        return row

    per = panel // W
    for p in range(n // panel):
        end = (p + 1) * per
        for q in range(0, per, 2):
            g, h = p * per + q, p * per + q + 1
            first, second = g * W, h * W
            scale, lower = pivots(column(g, first))
            cross = forward(column(h, first), scale, lower)
            crossed = {(k, s): spread(cross[s][k : k + 1, :]) for s in range(W) for k in range(W)}
            corner = column(h, second)
            for t in range(W):
                for s in range(W):
                    corner[t] = corner[t] - cross[s] * crossed[t, s]
            scale2, lower2 = pivots(corner)
            others = range(h + 1, end)
            left = {i: column(i, first) for i in others}
            right = {i: column(i, second) for i in others}
            solved, group = solve_rows(rows[g], first, scale, lower)
            rows[g] = group
            solved2, group2 = solve_rows(take(rows[h], cross, solved, first), second, scale2, lower2)
            rows[h] = group2
            for i in others:
                one = forward(left[i], scale, lower)
                two = right[i]
                for t in range(W):
                    for s in range(W):
                        two[t] = two[t] - one[s] * crossed[t, s]
                two = forward(two, scale2, lower2)
                rows[i] = take(take(rows[i], one, solved, first), two, solved2, second)
        if end < n // W:
            edge = end * W
            kept = lambda g: jnp.where((lane < (g + 1) * W) | (lane >= edge), rows[g], 0.0)
            done = jnp.concatenate([kept(g) for g in range(p * per, end)], axis=0)
            pair = split(done)
            term = joined(pair, pair, (0, 0))
            outside = (lane < p * panel) | (lane >= (p + 1) * panel)
            for i in range(end, n // W):
                rows[i] = jnp.where(outside, rows[i], 0.0) - term[W * i : W * (i + 1), :]
    out = jnp.concatenate(rows, axis=0)
    down = lax.broadcasted_iota(jnp.int32, (n, n), 0)
    across = lax.broadcasted_iota(jnp.int32, (n, n), 1)
    return jnp.where(down >= across, out, 0.0)


def plain(a, b):
    return lax.dot_general(a, b, (((1,), (0,)), ((), ())), preferred_element_type=jnp.float32)


def factor(work, high, low, beside=None):
    blocks, rows, order = work.shape
    down = lax.broadcasted_iota(jnp.int32, (rows, rows), 0)
    across = lax.broadcasted_iota(jnp.int32, (rows, rows), 1)
    unit = jnp.where(down == across, 1.0, 0.0)
    column_block = lax.broadcasted_iota(jnp.int32, (rows, order), 1) // rows

    def step(j, carry):
        at = pl.ds(pl.multiple_of(j * rows, rows), rows)
        if beside is not None:
            beside(j)
        inverse = factor_inverse(work[j, :, at])
        work[j, :, at] = unit
        solved = joined(split(inverse), split(work[j]), (1, 0))
        solved_high, solved_low = split(solved)
        high[at, :] = solved_high
        low[at, :] = solved_low
        for i in range(1, blocks):

            @pl.when(i > j)
            def _():
                cut = slice(i * rows, (i + 1) * rows)
                left = (high[at, cut].T, low[at, cut].T)
                work[i, :, at] = jnp.zeros((rows, rows), jnp.float32)
                work[i] = work[i] - joined(left, (solved_high, solved_low), (1, 0))

        keep = column_block <= j
        high[at, :] = jnp.where(keep, solved_high, 0.0).astype(jnp.bfloat16)
        low[at, :] = jnp.where(keep, solved_low, 0.0).astype(jnp.bfloat16)
        return carry

    lax.fori_loop(0, blocks, step, 0)


def solve(high, low, right_high, right_low, out_high, out_low, part, blocks):
    order = high.shape[0]
    rows = order // blocks
    across = slice(part * order, (part + 1) * order)
    for j in range(blocks):
        at, deep = slice(j * rows, (j + 1) * rows), (j + 1) * rows
        left = (high[at, :deep], low[at, :deep])
        top = right_high[:deep, across]
        if right_low is None:
            solved = plain(left[0], top) + plain(left[1], top)
        else:
            solved = joined(left, (top, right_low[:deep, across]), (1, 0))
        solved_high, solved_low = split(solved)
        out_high[at, across] = solved_high
        out_low[at, across] = solved_low


def flipped(place, bit):
    return place + bit - 2 * bit * ((place // bit) % 2)


class Spread:
    def __init__(self, size, place, view, send_sem, recv_sem, base=0, own=None):
        bits = [size >> (k + 1) for k in range(size.bit_length() - 1)]
        self.plan = [(b, 0) for b in bits]
        for k, b in enumerate(bits):
            earlier = [0]
            for e in bits[:k]:
                earlier += [m + e for m in earlier]
            self.plan += [(b, m) for m in earlier if m]
        self.source = {}
        for b, m in self.plan:
            if m:
                last = m & -m
                self.source[b, m] = self.plan.index((last, m - last))
        self.copies = []
        for k, (b, m) in enumerate(self.plan):
            held = place
            for e in bits:
                if m & e:
                    held = flipped(held, e)
            self.copies.append(
                pltpu.make_async_remote_copy(
                    src_ref=own if own is not None and m == 0 else view(held),
                    dst_ref=view(held),
                    send_sem=send_sem.at[base + k],
                    recv_sem=recv_sem.at[base + k],
                    device_id={"swath": flipped(place, b)},
                    device_id_type=MESH,
                )
            )

    def start_own(self):
        for copy, (b, m) in zip(self.copies, self.plan):
            if m == 0:
                copy.start()

    def forward(self):
        waited = set()
        for copy, item in zip(self.copies, self.plan):
            if item in self.source:
                source = self.source[item]
                if source not in waited:
                    self.copies[source].wait_recv()
                    waited.add(source)
                copy.start()

    def finish(self):
        waited = set(self.source.values())
        for k, copy in enumerate(self.copies):
            if k not in waited:
                copy.wait_recv()

    def sent(self):
        for copy in self.copies:
            copy.wait_send()


class Move:
    def __init__(self, source, target, send_sem, recv_sem, index, device, sends, receives):
        self.copy = pltpu.make_async_remote_copy(
            src_ref=source,
            dst_ref=target,
            send_sem=send_sem.at[index],
            recv_sem=recv_sem.at[index],
            device_id={"tm": device},
            device_id_type=MESH,
        )
        self.target, self.sends, self.receives = target, sends, receives

    def start(self):
        pl.when(self.sends)(self.copy.start)

    def receive(self):
        pl.when(self.receives)(self.copy.wait_recv)

        @pl.when(jnp.logical_not(self.receives))
        def _():
            self.target[...] = jnp.zeros(self.target.shape, self.target.dtype)

    def sent(self):
        pl.when(self.sends)(self.copy.wait_send)


def greet(times, size, place, me):
    barrier = pltpu.get_barrier_semaphore()
    count = jnp.int32(size - 1)
    for level in range(LEVELS):
        distance = 2**level
        for there, other in ((me >= distance, me - distance), (me + distance < times, me + distance)):

            @pl.when(there)
            def _():
                pl.semaphore_signal(barrier, inc=1, device_id={"tm": other}, device_id_type=MESH)

            count = count + there.astype(jnp.int32)
    for d in range(1, size):
        pl.semaphore_signal(
            barrier, inc=1, device_id={"swath": (place + d) % size}, device_id_type=MESH
        )
    return barrier, count


def pick(weighted, routes_ref, counts_ref, owner, slot):
    block_count = routes_ref.shape[1]
    place = jnp.int32(0)
    chosen = jnp.full((), -1, jnp.int32)
    for r in range(block_count):
        named = routes_ref[0, r] == owner
        live = r < counts_ref[0, 0]
        chosen = jnp.where(named & live & (place == slot), r, chosen)
        place = place + named.astype(jnp.int32)
    block = jnp.zeros(weighted[0].shape, jnp.float32)
    for r in range(block_count):
        block = jnp.where(chosen == r, weighted[r], block)
    return block.astype(jnp.bfloat16)


def kernel(times, size, total_slots, block_rows, design_ref, process_ref, prior_ref, routes_ref,
           counts_ref, out_diag_ref, out_coup_ref, obs, proc, leaving, prior, skew, work, high, low,
           right_high, right_low, solved_high, solved_low, parts, shares, land, terms, cross, corner,
           last_cross, last_full, last_half, first_send, first_recv, spread_send, spread_recv,
           prior_send, prior_recv, term_send, term_recv, cross_send, cross_recv, share_send,
           share_recv, part_send, part_recv, last_send, last_recv):
    place, me = lax.axis_index("swath"), lax.axis_index("tm")
    rows, order = process_ref.shape
    block_count = routes_ref.shape[1]
    slot_count = block_count // 2
    reach, half = size // 2, rows // 2
    hops = size - 1
    barrier, count = greet(times, size, place, me)

    weighted = []
    for r in range(block_count):
        raw = design_ref[r * block_rows : (r + 1) * block_rows, :].astype(jnp.float32)
        mean_sq = jnp.mean(raw * raw, axis=-1, keepdims=True)
        weighted.append(raw * lax.rsqrt(4.0 * total_slots * (mean_sq + 1e-06)))
    for slot in range(slot_count):
        cut = slice(slot * block_rows, (slot + 1) * block_rows)
        leaving[cut, :] = pick(weighted, routes_ref, counts_ref, me + 1, slot)
        obs[0, place, cut, :] = pick(weighted, routes_ref, counts_ref, me, slot)
    pl.semaphore_wait(barrier, count)

    behind, ahead = me >= 1, me + 1 < times
    spread = lambda view, k, own=None: Spread(
        size, place, view, spread_send, spread_recv, k * hops, own
    )
    slots = [pl.ds(c * block_rows, block_rows) for c in range(slot_count)]
    far_moves = [
        Move(process_ref, proc.at[1, place], first_send, first_recv, 0, me + 1, ahead, behind)
    ]
    for c, cut in enumerate(slots):
        far_moves.append(
            Move(leaving.at[cut], obs.at[1, place, cut], first_send, first_recv, c + 1, me + 1,
                 ahead, behind)
        )
    for move in far_moves:
        move.start()
    near_proc = spread(lambda held: proc.at[0, held], 0, process_ref)
    near_prior = Spread(size, place, lambda held: prior.at[held], prior_send, prior_recv, 0, prior_ref)
    near_obs = spread(lambda held: obs.at[0, held], 1)
    near_proc.start_own()
    near_prior.start_own()
    near_obs.start_own()
    proc[0, place] = process_ref[...]
    prior[place] = prior_ref[...]
    far_proc = spread(lambda held: proc.at[1, held], 2)
    far_obs = [
        spread(lambda held, cut=cut: obs.at[1, held, cut], 3 + c) for c, cut in enumerate(slots)
    ]
    far_moves[0].receive()
    far_proc.start_own()
    near_proc.forward()
    near_prior.forward()
    for c in range(slot_count):
        far_moves[c + 1].receive()
        far_obs[c].start_own()
    near_obs.forward()
    far_proc.forward()
    near_proc.finish()
    near_prior.finish()
    near_obs.finish()

    def gram(which, cut, b):
        total = None
        for i in range(size):
            term = lax.dot_general(
                obs[which, i, cut, b * rows : (b + 1) * rows],
                obs[which, i, cut, b * rows :],
                (((0,), (0,)), ((), ())),
                preferred_element_type=jnp.float32,
            )
            total = term if total is None else total + term
        return total

    square = (rows, rows)
    unit = lax.broadcasted_iota(jnp.int32, square, 0) == lax.broadcasted_iota(jnp.int32, square, 1)
    cuts = [slice(b * rows, (b + 1) * rows) for b in range(size)]
    for b in range(size):
        work[b, :, b * rows :] = gram(0, slice(None), b)
        work[b, :, cuts[b]] += jnp.where(unit, jnp.broadcast_to(prior[b][:1], square), 0.0)
        right_high[cuts[b], :order] = proc[0, b]
    far_proc.finish()
    both = lambda a, b: proc[0, a, :, cuts[b]].astype(jnp.float32) + proc[1, a, :, cuts[b]].astype(
        jnp.float32
    )
    for b in range(size):
        for q in range(size):
            right_high[cuts[b], order + q * rows : order + (q + 1) * rows] = proc[1, q, :, cuts[b]].T
            if q >= b:
                work[b, :, cuts[q]] += 0.5 * (both(b, q) + both(q, b).T)
    for c in range(slot_count):
        far_obs[c].forward()
        far_obs[c].finish()
        for b in range(size):
            work[b, :, b * rows :] += gram(1, slots[c], b)
    for s in range(size):

        @pl.when(place == s)
        def _():
            for d in range(reach):
                q = (s + d) % size
                block = work[s, :, cuts[q]] if q >= s else work[q, :, cuts[s]].T
                shares[0, s, d * rows : (d + 1) * rows] = block
            a, h = s % reach, s // reach
            shares[0, s, reach * rows :] = work[a, h * half : (h + 1) * half, cuts[a + reach]]

    piece = rows // size
    sending = []
    column = lambda part, b: pl.ds(pl.multiple_of(part * order + b * rows, rows), rows)
    share_cuts = [pl.ds(d * rows, rows) for d in range(reach)] + [pl.ds(reach * rows, half)]
    for level in range(LEVELS):
        distance = 2**level
        last = level == LEVELS - 1
        behind, ahead = me >= distance, me + distance < times
        if level == 0:
            factor(work, high, low)
        else:
            arrivals = parts.at[level - 1]
            below = 2 ** (level - 1)
            has_next = me + 2 * below <= times
            has_previous = me >= 2 * below

            def part_spread(c, arrivals=arrivals, level=level):
                cut = pl.ds(pl.multiple_of(c * piece, piece), piece)
                return Spread(
                    size, place, lambda held: arrivals.at[held, :, cut], part_send, part_recv,
                    ((level - 1) * size + c) * hops,
                )

            def beside(j, arrivals=arrivals, level=level, below=below, has_next=has_next,
                       has_previous=has_previous, part_spread=part_spread):
                cut = pl.ds(pl.multiple_of(j * piece, piece), piece)
                index = ((level - 1) * size + j) * 2
                Move(cross.at[level - 1, 0, cut], arrivals.at[place, 0, cut], cross_send, cross_recv,
                     index, me, has_next, has_next).receive()
                Move(cross.at[level - 1, 1, cut], arrivals.at[place, 1, cut], cross_send, cross_recv,
                     index + 1, me, has_previous, has_previous).receive()
                part_spread(j).start_own()

                @pl.when(j > 0)
                def _():
                    part_spread(j - 1).forward()

            factor(work, high, low, beside)
            part_spread(size - 1).forward()
            for c in range(size):
                part_spread(c).finish()
                sending.append(part_spread(c))
            for b in range(size):
                for part in range(2):
                    top, bottom = split(arrivals[b, part])
                    right_high[cuts[b], part * order : (part + 1) * order] = top
                    right_low[cuts[b], part * order : (part + 1) * order] = bottom

        lower = None if level == 0 else right_low
        term_moves, turned = [], []
        for part in range(2):
            solve(high, low, right_high, lower, solved_high, solved_low, part, size)
            pair = lambda b, part=part: (solved_high[:, column(part, b)], solved_low[:, column(part, b)])
            own = pair(place)
            own = (own[0].T, own[1].T)
            turned.append(own)
            wide = [pair((place + d) % size) for d in range(reach)]
            wide = tuple(jnp.concatenate([w[k] for w in wide], axis=1) for k in range(2))
            product = joined(own, wide, (1, 0))
            for d in range(reach):
                terms[level, part, d * rows : (d + 1) * rows] = product[:, d * rows : (d + 1) * rows]
            a, h = place % reach, place // reach
            first = pair(a)
            corner[...] = joined((first[0].T, first[1].T), pair(a + reach), (1, 0))
            terms[level, part, reach * rows :] = corner[pl.ds(pl.multiple_of(h * half, half), half), :]
            sends, receives = (ahead, behind) if part == 0 else (behind, ahead)
            for d, cut in enumerate(share_cuts):
                move = Move(
                    terms.at[level, part, cut], land.at[level, part, cut], term_send, term_recv,
                    (level * 2 + part) * len(share_cuts) + d,
                    me + distance if part == 0 else me - distance, sends, receives,
                )
                move.start()
                term_moves.append(move)

        cross_moves = []
        goes_down = behind & (me + distance <= times)
        comes_down = me + 2 * distance <= times
        whole = lambda part: (
            solved_high[:, part * order : (part + 1) * order],
            solved_low[:, part * order : (part + 1) * order],
        )
        cross[level, 0] = joined(turned[1], whole(0), (1, 0))
        if last:
            final = Move(
                cross.at[level, 0], last_cross, last_send, last_recv, 0, me - distance, goes_down,
                comes_down,
            )
            final.start()
        else:
            cross[level, 1] = joined(turned[0], whole(1), (1, 0))
            target = parts.at[level]
            for c in range(size):
                cut = pl.ds(c * piece, piece)
                index = (level * size + c) * 2
                cross_moves.append(
                    Move(cross.at[level, 0, cut], target.at[place, 0, cut], cross_send, cross_recv,
                         index, me - distance, goes_down, comes_down)
                )
                cross_moves.append(
                    Move(cross.at[level, 1, cut], target.at[place, 1, cut], cross_send, cross_recv,
                         index + 1, me + distance, behind & ahead, me >= 2 * distance)
                )
            for move in cross_moves:
                move.start()

        spreads = []
        for d, cut in enumerate(share_cuts):
            term_moves[d].receive()
            term_moves[len(share_cuts) + d].receive()
            shares[level + 1, place, cut] = (
                shares[level, place, cut] - land[level, 0, cut] - land[level, 1, cut]
            )
            if not last:
                spreads.append(
                    Spread(size, place, lambda held, cut=cut: shares.at[level + 1, held, cut],
                           share_send, share_recv, (level * len(share_cuts) + d) * hops)
                )
                spreads[-1].start_own()
        sending += term_moves + cross_moves + spreads
        if level == 0:
            mine = pl.ds(pl.multiple_of(place * rows, rows), rows)
            for q in range(size):
                there = proc[0, q, :, mine].astype(jnp.float32) + proc[1, q, :, mine].astype(jnp.float32)
                here = proc[0, place, :, cuts[q]].astype(jnp.float32) + proc[
                    1, place, :, cuts[q]
                ].astype(jnp.float32)
                skew[:, cuts[q]] = 0.5 * (here - there.T)
        if not last:
            for one in spreads:
                one.forward()
            for one in spreads:
                one.finish()
            held = shares.at[level + 1]
            for s in range(size):
                for d in range(reach):
                    q = (s + d) % size
                    block = held[s, d * rows : (d + 1) * rows]
                    if q >= s:
                        work[s, :, cuts[q]] = block
                    else:
                        work[q, :, cuts[s]] = block.T
                a, h = s % reach, s // reach
                work[a, h * half : (h + 1) * half, cuts[a + reach]] = held[s, reach * rows :]

    copies = []
    for d in range(1, reach):
        copies.append(
            pltpu.make_async_remote_copy(
                src_ref=shares.at[LEVELS, place, share_cuts[d]],
                dst_ref=last_full.at[d - 1],
                send_sem=last_send.at[d],
                recv_sem=last_recv.at[d],
                device_id={"swath": (place + d) % size},
                device_id_type=MESH,
            )
        )
    copies.append(
        pltpu.make_async_remote_copy(
            src_ref=shares.at[LEVELS, place, share_cuts[reach]],
            dst_ref=last_half,
            send_sem=last_send.at[reach],
            recv_sem=last_recv.at[reach],
            device_id={"swath": (place + reach) % size},
            device_id_type=MESH,
        )
    )
    for copy in copies:
        copy.start()
    final.receive()
    out_coup_ref[...] = -last_cross[...]
    for copy in copies:
        copy.wait_recv()
    for s in range(size):

        @pl.when(place == s)
        def _():
            own = shares.at[LEVELS, s]
            for d in range(reach):
                q = (s + d) % size
                out_diag_ref[:, cuts[q]] = own[d * rows : (d + 1) * rows] + skew[:, cuts[q]]
            for d in range(1, reach):
                q = (s - d) % size
                out_diag_ref[:, cuts[q]] = last_full[d - 1].T + skew[:, cuts[q]]
            pieces = [own[reach * rows :], last_half[...]]
            if s < reach:
                block = jnp.concatenate(pieces, axis=0)
            else:
                block = jnp.concatenate(pieces[::-1], axis=0).T
            q = (s + reach) % size
            out_diag_ref[:, cuts[q]] = block + skew[:, cuts[q]]

    for copy in copies:
        copy.wait_send()
    final.sent()
    for move in far_moves + sending:
        move.sent()
    for one in [near_proc, near_prior, near_obs, far_proc] + far_obs:
        one.sent()


def shards(design, process, prior_prec, routes, counts):
    times, size = lax.axis_size("tm"), lax.axis_size("swath")
    rows, order = process.shape[1:]
    block_count = routes.shape[1]
    block_rows = design.shape[1] // block_count
    slot_count = block_count // 2
    observed = slot_count * block_rows
    total_slots = 2 * observed * size
    share = rows * (size // 2) + rows // 2
    hops = size - 1
    kinds = size // 2 + 1
    prior = jnp.broadcast_to(prior_prec, (8, rows))
    vmem, smem = (pl.BlockSpec(memory_space=m) for m in (pltpu.VMEM, pltpu.SMEM))
    f32, bf16 = jnp.float32, jnp.bfloat16
    dma = lambda n: [pltpu.SemaphoreType.DMA((n,))] * 2
    diag_rows, coup_rows = pl.pallas_call(
        functools.partial(kernel, times, size, total_slots, block_rows),
        out_shape=(jax.ShapeDtypeStruct((rows, order), f32),) * 2,
        in_specs=[vmem, vmem, vmem, smem, smem],
        out_specs=(vmem,) * 2,
        scratch_shapes=[
            pltpu.VMEM((2, size, observed, order), bf16),
            pltpu.VMEM((2, size, rows, order), bf16),
            pltpu.VMEM((observed, order), bf16),
            pltpu.VMEM((size,) + prior.shape, f32),
            pltpu.VMEM((rows, order), f32),
            pltpu.VMEM((size, rows, order), f32),
            pltpu.VMEM((order, order), bf16),
            pltpu.VMEM((order, order), bf16),
            pltpu.VMEM((order, 2 * order), bf16),
            pltpu.VMEM((order, 2 * order), bf16),
            pltpu.VMEM((order, 2 * order), bf16),
            pltpu.VMEM((order, 2 * order), bf16),
            pltpu.VMEM((LEVELS - 1, size, 2, rows, order), f32),
            pltpu.VMEM((LEVELS + 1, size, share, rows), f32),
            pltpu.VMEM((LEVELS, 2, share, rows), f32),
            pltpu.VMEM((LEVELS, 2, share, rows), f32),
            pltpu.VMEM((LEVELS, 2, rows, order), f32),
            pltpu.VMEM((rows, rows), f32),
            pltpu.VMEM((rows, order), f32),
            pltpu.VMEM((max(size // 2 - 1, 1), rows, rows), f32),
            pltpu.VMEM((rows // 2, rows), f32),
        ]
        + dma(1 + slot_count)
        + dma((3 + slot_count) * hops)
        + dma(hops)
        + dma(LEVELS * 2 * kinds)
        + dma((LEVELS - 1) * size * 2)
        + dma((LEVELS - 1) * kinds * hops)
        + dma((LEVELS - 1) * size * hops)
        + dma(kinds),
        compiler_params=pltpu.CompilerParams(collective_id=0, has_side_effects=True),
    )(design[0], process[0], prior, routes, counts)
    return (diag_rows[None], coup_rows[None])


def solution(mesh):
    return jax.shard_map(
        shards,
        mesh=mesh,
        in_specs=(
            P("tm", "swath", None),
            P("tm", "swath", None),
            P("tm", "swath"),
            P("tm", "swath"),
            P("tm", "swath"),
        ),
        out_specs=(P("tm", "swath", None), P("tm", "swath", None)),
        check_vma=False,
    )
```

time: 166 us -> 135 us (0.81)
  Pallas kernels: 161 us -> 130 us
    pallas_call x5 -> x1, Pallas kernels: 161 us -> 130 us  [shards(): pl.pallas_call(functools.partial(kernel, times, size, total_slots, block_...]
where the time goes in v2:
time: 135 us
  Pallas kernels  130 us (96%)
  local copies, waits for them, and re-layouts  3.66 us (3%)
    pallas_call x1, Pallas kernels, shards(): pl.pallas_call(functools.partial(kernel, times, size, total_slots, block_...  130 us
    unnamed x6, local copies, waits for them, and re-layouts  3.07 us

profile of v2, /device:TPU:0, one launch (start us, length us, event | category | flops | bytes accessed | tf_op | source)
XLA Modules:
  0.0 134.7 jit_solution(8968305537694175490)
XLA Ops:
  1.3 0.0 copy-start.1
  1.3 0.6 copy-done.1
  1.9 0.6 broadcast_in_dim.14.prior_ref
  2.5 129.7 %shard_map.68 = (f32[128,512]{1,0:T(8,128)}, f32[128,512]{1,0:T(8,128)}) custom-call(bf16[512,512]{1,0:T(8,128)(2,1)} %bitcast.5, bf16[128,512]{1,0:T(8,128)(2,1)} %bitcast.8, f32[8,128]{1,0:T(8,128)} %broadcast_in_dim.14.prior_ref, s32[1,4]{1,0:T(1,128)} %routes_ref.1, s32[1,1]{1,0:T(1,128)S(6)} %copy.9.counts_ref), custom_call_target="tpu_custom_call" | custom-call | tf_op jit(solution)/shard_map/pallas_call | solution.py:625
  132.3 0.0 copy-start
  132.3 1.7 %copy.10 = f32[1,128,512]{2,1,0:T(8,128)} copy(f32[1,128,512]{2,1,0:T(8,128)} %bitcast.7) | data formatting | bytes 524288
  134.0 0.0 copy-done
  134.0 0.7 copy.11
Async XLA Ops:
  1.3 0.7 copy-start.1
  132.3 1.7 %copy-start = (f32[128,512]{1,0:T(8,128)S(1)}, f32[128,512]{1,0:T(8,128)}, u32[]{:S(2)}) copy-start(f32[128,512]{1,0:T(8,128)} %get-tuple-element.5) | copy-start | bytes 786436

commit v3 on v2

--- a/solution.py
+++ b/solution.py
@@ -9,6 +9,7 @@
 
 LEVELS = 3
 W = 8
+PLAN = (((0, 3), (2, 5), (4, 7), (5, 8)), ((0, 3), (1, 5), (2, 6), (3, 7)))
 MESH = pl.DeviceIdType.MESH
 
 
@@ -135,8 +136,10 @@
     def step(j, carry):
         at = pl.ds(pl.multiple_of(j * rows, rows), rows)
         if beside is not None:
-            beside(j)
+            beside(j, 0)
         inverse = factor_inverse(work[j, :, at])
+        if beside is not None:
+            beside(j, 1)
         work[j, :, at] = unit
         solved = joined(split(inverse), split(work[j]), (1, 0))
         solved_high, solved_low = split(solved)
@@ -298,10 +301,10 @@
 
 
 def kernel(times, size, total_slots, block_rows, design_ref, process_ref, prior_ref, routes_ref,
-           counts_ref, out_diag_ref, out_coup_ref, obs, proc, leaving, prior, skew, work, high, low,
+           counts_ref, out_diag_ref, out_coup_ref, skew, obs, proc, leaving, prior, work, high, low,
            right_high, right_low, solved_high, solved_low, parts, shares, land, terms, cross, corner,
            last_cross, last_full, last_half, first_send, first_recv, spread_send, spread_recv,
-           prior_send, prior_recv, term_send, term_recv, cross_send, cross_recv, share_send,
+           prior_send, prior_recv, inner_send, inner_recv, term_send, term_recv, cross_send, cross_recv, share_send,
            share_recv, part_send, part_recv, last_send, last_recv):
     place, me = lax.axis_index("swath"), lax.axis_index("tm")
     rows, order = process_ref.shape
@@ -311,6 +314,38 @@
     hops = size - 1
     barrier, count = greet(times, size, place, me)
 
+    behind, ahead = me >= 1, me + 1 < times
+    other = flipped(place, reach)
+    spread = lambda view, k, own=None: Spread(
+        size, place, view, spread_send, spread_recv, k * hops, own
+    )
+    inner = lambda view, k: Spread(reach, place, view, inner_send, inner_recv, k * (reach - 1))
+    slots = [pl.ds(c * block_rows, block_rows) for c in range(slot_count)]
+    far_move = lambda source, target, k: Move(
+        source, target, first_send, first_recv, k, me + 1, ahead, behind
+    )
+    far_moves = [
+        far_move(process_ref, proc.at[1, place], 0),
+        far_move(proc.at[0, other], proc.at[1, other], 1),
+    ]
+    for c, cut in enumerate(slots):
+        far_moves.append(far_move(leaving.at[cut], obs.at[1, place, cut], c + 2))
+    near_proc = spread(lambda held: proc.at[0, held], 0, process_ref)
+    near_prior = Spread(size, place, lambda held: prior.at[held], prior_send, prior_recv)
+    near_obs = spread(lambda held: obs.at[0, held], 1)
+    far_procs = [
+        inner(lambda held: proc.at[1, held], 0),
+        inner(lambda held: proc.at[1, flipped(held, reach)], 1),
+    ]
+    far_obs = [
+        spread(lambda held, cut=cut: obs.at[1, held, cut], 2 + c) for c, cut in enumerate(slots)
+    ]
+    prior[place] = jnp.broadcast_to(prior_ref[...], prior.shape[1:])
+    pl.semaphore_wait(barrier, count)
+    far_moves[0].start()
+    near_proc.start_own()
+    proc[0, place] = process_ref[...]
+
     weighted = []
     for r in range(block_count):
         raw = design_ref[r * block_rows : (r + 1) * block_rows, :].astype(jnp.float32)
@@ -318,49 +353,27 @@
         weighted.append(raw * lax.rsqrt(4.0 * total_slots * (mean_sq + 1e-06)))
     for slot in range(slot_count):
         cut = slice(slot * block_rows, (slot + 1) * block_rows)
+        obs[0, place, cut, :] = pick(weighted, routes_ref, counts_ref, me, slot)
+    near_obs.start_own()
+    for slot in range(slot_count):
+        cut = slice(slot * block_rows, (slot + 1) * block_rows)
         leaving[cut, :] = pick(weighted, routes_ref, counts_ref, me + 1, slot)
-        obs[0, place, cut, :] = pick(weighted, routes_ref, counts_ref, me, slot)
-    pl.semaphore_wait(barrier, count)
-
-    behind, ahead = me >= 1, me + 1 < times
-    spread = lambda view, k, own=None: Spread(
-        size, place, view, spread_send, spread_recv, k * hops, own
-    )
-    slots = [pl.ds(c * block_rows, block_rows) for c in range(slot_count)]
-    far_moves = [
-        Move(process_ref, proc.at[1, place], first_send, first_recv, 0, me + 1, ahead, behind)
-    ]
-    for c, cut in enumerate(slots):
-        far_moves.append(
-            Move(leaving.at[cut], obs.at[1, place, cut], first_send, first_recv, c + 1, me + 1,
-                 ahead, behind)
-        )
-    for move in far_moves:
-        move.start()
-    near_proc = spread(lambda held: proc.at[0, held], 0, process_ref)
-    near_prior = Spread(size, place, lambda held: prior.at[held], prior_send, prior_recv, 0, prior_ref)
-    near_obs = spread(lambda held: obs.at[0, held], 1)
-    near_proc.start_own()
+        far_moves[slot + 2].start()
     near_prior.start_own()
-    near_obs.start_own()
-    proc[0, place] = process_ref[...]
-    prior[place] = prior_ref[...]
-    far_proc = spread(lambda held: proc.at[1, held], 2)
-    far_obs = [
-        spread(lambda held, cut=cut: obs.at[1, held, cut], 3 + c) for c, cut in enumerate(slots)
-    ]
+    near_proc.forward()
+    far_moves[1].start()
     far_moves[0].receive()
-    far_proc.start_own()
-    near_proc.forward()
+    far_procs[0].start_own()
     near_prior.forward()
     for c in range(slot_count):
-        far_moves[c + 1].receive()
+        far_moves[c + 2].receive()
         far_obs[c].start_own()
     near_obs.forward()
-    far_proc.forward()
     near_proc.finish()
     near_prior.finish()
     near_obs.finish()
+    far_moves[1].receive()
+    far_procs[1].start_own()
 
     def gram(which, cut, b):
         total = None
@@ -381,7 +394,9 @@
         work[b, :, b * rows :] = gram(0, slice(None), b)
         work[b, :, cuts[b]] += jnp.where(unit, jnp.broadcast_to(prior[b][:1], square), 0.0)
         right_high[cuts[b], :order] = proc[0, b]
-    far_proc.finish()
+    for one in far_procs:
+        one.forward()
+        one.finish()
     both = lambda a, b: proc[0, a, :, cuts[b]].astype(jnp.float32) + proc[1, a, :, cuts[b]].astype(
         jnp.float32
     )
@@ -422,46 +437,72 @@
             has_next = me + 2 * below <= times
             has_previous = me >= 2 * below
 
-            def part_spread(c, arrivals=arrivals, level=level):
-                cut = pl.ds(pl.multiple_of(c * piece, piece), piece)
-                return Spread(
-                    size, place, lambda held: arrivals.at[held, :, cut], part_send, part_recv,
-                    ((level - 1) * size + c) * hops,
+            part_spreads, part_moves = [], []
+            for c in range(size):
+                cut = pl.ds(c * piece, piece)
+                index = ((level - 1) * size + c) * 2
+                part_spreads.append(
+                    Spread(
+                        size, place, lambda held, cut=cut: arrivals.at[held, :, cut], part_send,
+                        part_recv, ((level - 1) * size + c) * hops,
+                    )
                 )
-
-            def beside(j, arrivals=arrivals, level=level, below=below, has_next=has_next,
-                       has_previous=has_previous, part_spread=part_spread):
-                cut = pl.ds(pl.multiple_of(j * piece, piece), piece)
-                index = ((level - 1) * size + j) * 2
-                Move(cross.at[level - 1, 0, cut], arrivals.at[place, 0, cut], cross_send, cross_recv,
-                     index, me, has_next, has_next).receive()
-                Move(cross.at[level - 1, 1, cut], arrivals.at[place, 1, cut], cross_send, cross_recv,
-                     index + 1, me, has_previous, has_previous).receive()
-                part_spread(j).start_own()
-
-                @pl.when(j > 0)
-                def _():
-                    part_spread(j - 1).forward()
+                part_moves.append([
+                    Move(cross.at[level - 1, k, cut], arrivals.at[place, k, cut], cross_send,
+                         cross_recv, index + k, me, there, there)
+                    for k, there in enumerate((has_next, has_previous))
+                ])
+
+            def beside(j, late):
+                if late:
+                    pl.when(j == 0)(pending)
+                for c in range(size):
+                    land_at, pass_at = PLAN[min(level, 2) - 1][c % 4]
+                    if land_at % 2 == late:
+
+                        @pl.when(j == land_at // 2)
+                        def _():
+                            for move in part_moves[c]:
+                                move.receive()
+                            part_spreads[c].start_own()
+
+                    if pass_at % 2 == late:
+                        pl.when(j == pass_at // 2)(part_spreads[c].forward)
 
             factor(work, high, low, beside)
-            part_spread(size - 1).forward()
             for c in range(size):
-                part_spread(c).finish()
-                sending.append(part_spread(c))
+                if PLAN[min(level, 2) - 1][c % 4][1] >= 2 * size:
+                    part_spreads[c].forward()
+            for one in part_spreads:
+                one.finish()
+            sending += part_spreads
             for b in range(size):
                 for part in range(2):
                     top, bottom = split(arrivals[b, part])
                     right_high[cuts[b], part * order : (part + 1) * order] = top
                     right_low[cuts[b], part * order : (part + 1) * order] = bottom
 
+        goes_down = behind & (me + distance <= times)
+        comes_down = me + 2 * distance <= times
+        whole = lambda part: (
+            solved_high[:, part * order : (part + 1) * order],
+            solved_low[:, part * order : (part + 1) * order],
+        )
         lower = None if level == 0 else right_low
-        term_moves, turned = [], []
-        for part in range(2):
+        term_moves, turned = [None, None], [None, None]
+        for part in (1, 0) if last else (0, 1):
             solve(high, low, right_high, lower, solved_high, solved_low, part, size)
             pair = lambda b, part=part: (solved_high[:, column(part, b)], solved_low[:, column(part, b)])
             own = pair(place)
             own = (own[0].T, own[1].T)
-            turned.append(own)
+            turned[part] = own
+            if last and part == 0:
+                cross[level, 0] = joined(turned[1], whole(0), (1, 0))
+                final = Move(
+                    cross.at[level, 0], last_cross, last_send, last_recv, 0, me - distance, goes_down,
+                    comes_down,
+                )
+                final.start()
             wide = [pair((place + d) % size) for d in range(reach)]
             wide = tuple(jnp.concatenate([w[k] for w in wide], axis=1) for k in range(2))
             product = joined(own, wide, (1, 0))
@@ -472,6 +513,7 @@
             corner[...] = joined((first[0].T, first[1].T), pair(a + reach), (1, 0))
             terms[level, part, reach * rows :] = corner[pl.ds(pl.multiple_of(h * half, half), half), :]
             sends, receives = (ahead, behind) if part == 0 else (behind, ahead)
+            moves = []
             for d, cut in enumerate(share_cuts):
                 move = Move(
                     terms.at[level, part, cut], land.at[level, part, cut], term_send, term_recv,
@@ -479,23 +521,12 @@
                     me + distance if part == 0 else me - distance, sends, receives,
                 )
                 move.start()
-                term_moves.append(move)
+                moves.append(move)
+            term_moves[part] = moves
 
         cross_moves = []
-        goes_down = behind & (me + distance <= times)
-        comes_down = me + 2 * distance <= times
-        whole = lambda part: (
-            solved_high[:, part * order : (part + 1) * order],
-            solved_low[:, part * order : (part + 1) * order],
-        )
-        cross[level, 0] = joined(turned[1], whole(0), (1, 0))
-        if last:
-            final = Move(
-                cross.at[level, 0], last_cross, last_send, last_recv, 0, me - distance, goes_down,
-                comes_down,
-            )
-            final.start()
-        else:
+        if not last:
+            cross[level, 0] = joined(turned[1], whole(0), (1, 0))
             cross[level, 1] = joined(turned[0], whole(1), (1, 0))
             target = parts.at[level]
             for c in range(size):
@@ -514,8 +545,8 @@
 
         spreads = []
         for d, cut in enumerate(share_cuts):
-            term_moves[d].receive()
-            term_moves[len(share_cuts) + d].receive()
+            term_moves[0][d].receive()
+            term_moves[1][d].receive()
             shares[level + 1, place, cut] = (
                 shares[level, place, cut] - land[level, 0, cut] - land[level, 1, cut]
             )
@@ -525,7 +556,9 @@
                            share_send, share_recv, (level * len(share_cuts) + d) * hops)
                 )
                 spreads[-1].start_own()
-        sending += term_moves + cross_moves + spreads
+                if d == len(share_cuts) - 2:
+                    spreads[0].forward()
+        sending += term_moves[0] + term_moves[1] + cross_moves + spreads
         if level == 0:
             mine = pl.ds(pl.multiple_of(place * rows, rows), rows)
             for q in range(size):
@@ -535,21 +568,26 @@
                 ].astype(jnp.float32)
                 skew[:, cuts[q]] = 0.5 * (here - there.T)
         if not last:
-            for one in spreads:
-                one.forward()
-            for one in spreads:
-                one.finish()
+            spreads[0].finish()
             held = shares.at[level + 1]
             for s in range(size):
-                for d in range(reach):
-                    q = (s + d) % size
-                    block = held[s, d * rows : (d + 1) * rows]
-                    if q >= s:
-                        work[s, :, cuts[q]] = block
-                    else:
-                        work[q, :, cuts[s]] = block.T
-                a, h = s % reach, s // reach
-                work[a, h * half : (h + 1) * half, cuts[a + reach]] = held[s, reach * rows :]
+                work[s, :, cuts[s]] = held[s, :rows]
+
+            def pending(spreads=spreads, held=held):
+                for one in spreads[1:]:
+                    one.forward()
+                for one in spreads[1:]:
+                    one.finish()
+                for s in range(size):
+                    for d in range(1, reach):
+                        q = (s + d) % size
+                        block = held[s, d * rows : (d + 1) * rows]
+                        if q >= s:
+                            work[s, :, cuts[q]] = block
+                        else:
+                            work[q, :, cuts[s]] = block.T
+                    a, h = s % reach, s // reach
+                    work[a, h * half : (h + 1) * half, cuts[a + reach]] = held[s, reach * rows :]
 
     copies = []
     for d in range(1, reach):
@@ -576,7 +614,7 @@
     for copy in copies:
         copy.start()
     final.receive()
-    out_coup_ref[...] = -last_cross[...]
+    out_coup_ref[...] = last_cross[...]
     for copy in copies:
         copy.wait_recv()
     for s in range(size):
@@ -586,24 +624,24 @@
             own = shares.at[LEVELS, s]
             for d in range(reach):
                 q = (s + d) % size
-                out_diag_ref[:, cuts[q]] = own[d * rows : (d + 1) * rows] + skew[:, cuts[q]]
+                out_diag_ref[:, cuts[q]] = own[d * rows : (d + 1) * rows]
             for d in range(1, reach):
                 q = (s - d) % size
-                out_diag_ref[:, cuts[q]] = last_full[d - 1].T + skew[:, cuts[q]]
+                out_diag_ref[:, cuts[q]] = last_full[d - 1].T
             pieces = [own[reach * rows :], last_half[...]]
             if s < reach:
                 block = jnp.concatenate(pieces, axis=0)
             else:
                 block = jnp.concatenate(pieces[::-1], axis=0).T
             q = (s + reach) % size
-            out_diag_ref[:, cuts[q]] = block + skew[:, cuts[q]]
+            out_diag_ref[:, cuts[q]] = block
 
     for copy in copies:
         copy.wait_send()
     final.sent()
     for move in far_moves + sending:
         move.sent()
-    for one in [near_proc, near_prior, near_obs, far_proc] + far_obs:
+    for one in [near_proc, near_prior, near_obs] + far_procs + far_obs:
         one.sent()
 
 
@@ -618,21 +656,19 @@
     share = rows * (size // 2) + rows // 2
     hops = size - 1
     kinds = size // 2 + 1
-    prior = jnp.broadcast_to(prior_prec, (8, rows))
     vmem, smem = (pl.BlockSpec(memory_space=m) for m in (pltpu.VMEM, pltpu.SMEM))
     f32, bf16 = jnp.float32, jnp.bfloat16
     dma = lambda n: [pltpu.SemaphoreType.DMA((n,))] * 2
-    diag_rows, coup_rows = pl.pallas_call(
+    diag_rows, coup_rows, skew = pl.pallas_call(
         functools.partial(kernel, times, size, total_slots, block_rows),
-        out_shape=(jax.ShapeDtypeStruct((rows, order), f32),) * 2,
+        out_shape=(jax.ShapeDtypeStruct((rows, order), f32),) * 3,
         in_specs=[vmem, vmem, vmem, smem, smem],
-        out_specs=(vmem,) * 2,
+        out_specs=(vmem,) * 3,
         scratch_shapes=[
             pltpu.VMEM((2, size, observed, order), bf16),
             pltpu.VMEM((2, size, rows, order), bf16),
             pltpu.VMEM((observed, order), bf16),
-            pltpu.VMEM((size,) + prior.shape, f32),
-            pltpu.VMEM((rows, order), f32),
+            pltpu.VMEM((size, 8, rows), f32),
             pltpu.VMEM((size, rows, order), f32),
             pltpu.VMEM((order, order), bf16),
             pltpu.VMEM((order, order), bf16),
@@ -650,17 +686,18 @@
             pltpu.VMEM((max(size // 2 - 1, 1), rows, rows), f32),
             pltpu.VMEM((rows // 2, rows), f32),
         ]
-        + dma(1 + slot_count)
-        + dma((3 + slot_count) * hops)
+        + dma(2 + slot_count)
+        + dma((2 + slot_count) * hops)
         + dma(hops)
+        + dma(2 * (size // 2 - 1))
         + dma(LEVELS * 2 * kinds)
         + dma((LEVELS - 1) * size * 2)
         + dma((LEVELS - 1) * kinds * hops)
         + dma((LEVELS - 1) * size * hops)
         + dma(kinds),
         compiler_params=pltpu.CompilerParams(collective_id=0, has_side_effects=True),
-    )(design[0], process[0], prior, routes, counts)
-    return (diag_rows[None], coup_rows[None])
+    )(design[0], process[0], prior_prec, routes, counts)
+    return ((diag_rows + skew)[None], -coup_rows[None])
 
 
 def solution(mesh):

time: 135 us -> 124 us (0.919)
  Pallas kernels: 130 us -> 121 us
  local copies, waits for them, and re-layouts: 3.66 us -> 0 us
  other arithmetic: 0 us -> 1.96 us
    pallas_call x1, Pallas kernels: 130 us -> 121 us  [shards(): pl.pallas_call(functools.partial(kernel, times, size, total_slots, block_...]
    unnamed x6 -> x0, local copies, waits for them, and re-layouts: 3.07 us -> none
    neg x0 -> x1, other arithmetic: none -> 1.96 us  [shards(): return ((diag_rows + skew)[None], -coup_rows[None])]
where the time goes in v3:
time: 124 us
  Pallas kernels  121 us (98%)
  other arithmetic  1.96 us (2%)
  between operations  1.29 us (1%)
    pallas_call x1, Pallas kernels, shards(): pl.pallas_call(functools.partial(kernel, times, size, total_slots, block_...  121 us

profile of v3, /device:TPU:0, one launch (start us, length us, event | category | flops | bytes accessed | tf_op | source)
XLA Modules:
  0.0 123.8 jit_solution(6712099075262503417)
XLA Ops:
  1.3 120.6 %shard_map.68 = (f32[128,512]{1,0:T(8,128)}, f32[128,512]{1,0:T(8,128)}, f32[128,512]{1,0:T(8,128)}) custom-call(bf16[512,512]{1,0:T(8,128)(2,1)} %bitcast.6, bf16[128,512]{1,0:T(8,128)(2,1)} %bitcast.7, f32[1,128]{1,0:T(1,128)} %prior_ref.1, s32[1,4]{1,0:T(1,128)} %routes_ref.1, s32[1,1]{1,0:T(1,128)S(6)} %copy.7.counts_ref), custom_call_target="tpu_custom_call" | custom-call | tf_op jit(solution)/shard_map/pallas_call | solution.py:662
  121.8 2.0 %negate_bitcast_fusion = (f32[1,128,512]{2,1,0:T(8,128)}, f32[1,128,512]{2,1,0:T(8,128)}) fusion(f32[128,512]{1,0:T(8,128)} %get-tuple-element.7, f32[128,512]{1,0:T(8,128)} %get-tuple-element.5, f32[128,512]{1,0:T(8,128)} %get-tuple-element.6), kind=kLoop, calls=%fused_computation | loop fusion | flops 131072 | bytes 1310720 | tf_op jit(solution)/shard_map/neg | solution.py:700

commit v4 on v3

--- a/solution.py
+++ b/solution.py
@@ -9,7 +9,11 @@
 
 LEVELS = 3
 W = 8
-PLAN = (((0, 3), (2, 5), (4, 7), (5, 8)), ((0, 3), (1, 5), (2, 6), (3, 7)))
+SHARES = ((5, 5, 4, 2), (3, 5, 4, 4))
+PLAN = (
+    ((1, 3, 3, 6), (2, 4, 4, 7), (3, 5, 5, 8), (3, 5, 6, 8)),
+    ((0, 3), (1, 5), (2, 6), (3, 7)),
+)
 MESH = pl.DeviceIdType.MESH
 
 
@@ -122,8 +126,10 @@
     return jnp.where(down >= across, out, 0.0)
 
 
-def plain(a, b):
-    return lax.dot_general(a, b, (((1,), (0,)), ((), ())), preferred_element_type=jnp.float32)
+def plain(a, b, dims):
+    return lax.dot_general(
+        a, b, (((dims[0],), (dims[1],)), ((), ())), preferred_element_type=jnp.float32
+    )
 
 
 def factor(work, high, low, beside=None):
@@ -162,18 +168,19 @@
     lax.fori_loop(0, blocks, step, 0)
 
 
-def solve(high, low, right_high, right_low, out_high, out_low, part, blocks):
+def solve(high, low, right_high, right_low, out_high, out_low, part, blocks, turn):
     order = high.shape[0]
     rows = order // blocks
     across = slice(part * order, (part + 1) * order)
     for j in range(blocks):
         at, deep = slice(j * rows, (j + 1) * rows), (j + 1) * rows
         left = (high[at, :deep], low[at, :deep])
-        top = right_high[:deep, across]
+        at_right = (slice(None), slice(part * order, part * order + deep)) if turn else (slice(deep), across)
+        dims = (1, 1) if turn else (1, 0)
         if right_low is None:
-            solved = plain(left[0], top) + plain(left[1], top)
+            solved = plain(left[0], right_high[at_right], dims) + plain(left[1], right_high[at_right], dims)
         else:
-            solved = joined(left, (top, right_low[:deep, across]), (1, 0))
+            solved = joined(left, (right_high[at_right], right_low[at_right]), dims)
         solved_high, solved_low = split(solved)
         out_high[at, across] = solved_high
         out_low[at, across] = solved_low
@@ -266,6 +273,12 @@
         pl.when(self.sends)(self.copy.wait_send)
 
 
+def band_cuts(rows, count, level):
+    shares = SHARES[min(level, 1)] if count == 4 else (16 // count,) * count
+    sizes = [rows * share // 16 for share in shares]
+    return [pl.ds(sum(sizes[:c]), size) for c, size in enumerate(sizes)]
+
+
 def greet(times, size, place, me):
     barrier = pltpu.get_barrier_semaphore()
     count = jnp.int32(size - 1)
@@ -305,7 +318,7 @@
            right_high, right_low, solved_high, solved_low, parts, shares, land, terms, cross, corner,
            last_cross, last_full, last_half, first_send, first_recv, spread_send, spread_recv,
            prior_send, prior_recv, inner_send, inner_recv, term_send, term_recv, cross_send, cross_recv, share_send,
-           share_recv, part_send, part_recv, last_send, last_recv):
+           share_recv, part_send, part_recv, relay_send, relay_recv, again_send, again_recv, last_send, last_recv):
     place, me = lax.axis_index("swath"), lax.axis_index("tm")
     rows, order = process_ref.shape
     block_count = routes_ref.shape[1]
@@ -372,8 +385,6 @@
     near_proc.finish()
     near_prior.finish()
     near_obs.finish()
-    far_moves[1].receive()
-    far_procs[1].start_own()
 
     def gram(which, cut, b):
         total = None
@@ -394,6 +405,9 @@
         work[b, :, b * rows :] = gram(0, slice(None), b)
         work[b, :, cuts[b]] += jnp.where(unit, jnp.broadcast_to(prior[b][:1], square), 0.0)
         right_high[cuts[b], :order] = proc[0, b]
+    far_moves[1].receive()
+    far_procs[1].start_own()
+    far_obs[0].forward()
     for one in far_procs:
         one.forward()
         one.finish()
@@ -401,13 +415,14 @@
         jnp.float32
     )
     for b in range(size):
+        right_high[cuts[b], order:] = proc[1, b]
         for q in range(size):
-            right_high[cuts[b], order + q * rows : order + (q + 1) * rows] = proc[1, q, :, cuts[b]].T
             if q >= b:
                 work[b, :, cuts[q]] += 0.5 * (both(b, q) + both(q, b).T)
     for c in range(slot_count):
-        far_obs[c].forward()
         far_obs[c].finish()
+        if c + 1 < slot_count:
+            far_obs[c + 1].forward()
         for b in range(size):
             work[b, :, b * rows :] += gram(1, slots[c], b)
     for s in range(size):
@@ -421,7 +436,7 @@
             a, h = s % reach, s // reach
             shares[0, s, reach * rows :] = work[a, h * half : (h + 1) * half, cuts[a + reach]]
 
-    piece = rows // size
+    bands = [band_cuts(rows, size, level) for level in range(LEVELS)]
     sending = []
     column = lambda part, b: pl.ds(pl.multiple_of(part * order + b * rows, rows), rows)
     share_cuts = [pl.ds(d * rows, rows) for d in range(reach)] + [pl.ds(reach * rows, half)]
@@ -437,45 +452,69 @@
             has_next = me + 2 * below <= times
             has_previous = me >= 2 * below
 
-            part_spreads, part_moves = [], []
+            part_spreads, relays, actions = [], [], [(1, pending)]
             for c in range(size):
-                cut = pl.ds(c * piece, piece)
-                index = ((level - 1) * size + c) * 2
-                part_spreads.append(
-                    Spread(
-                        size, place, lambda held, cut=cut: arrivals.at[held, :, cut], part_send,
-                        part_recv, ((level - 1) * size + c) * hops,
+                cut = bands[level - 1][c]
+                base = ((level - 1) * size + c) * hops
+                kinds = (has_next, has_previous)
+                arrive = [
+                    Move(cross.at[level - 1, k, cut], arrivals.at[place, k, cut], cross_send,
+                         cross_recv, ((level - 1) * size + c) * 2 + k, me, kinds[k], kinds[k])
+                    for k in range(2)
+                ]
+                if level == 1:
+                    relay = Move(
+                        arrivals.at[place, 0, cut], arrivals.at[place, 1, cut], relay_send, relay_recv,
+                        c, me + 2 * below, me + 2 * below < times, has_previous,
                     )
-                )
-                part_moves.append([
-                    Move(cross.at[level - 1, k, cut], arrivals.at[place, k, cut], cross_send,
-                         cross_recv, index + k, me, there, there)
-                    for k, there in enumerate((has_next, has_previous))
-                ])
+                    pair_of = [
+                        Spread(size, place, lambda held, cut=cut, k=k: arrivals.at[held, k, cut],
+                               sems[0], sems[1], first)
+                        for k, sems, first in (
+                            (0, (part_send, part_recv), base),
+                            (1, (again_send, again_recv), c * hops),
+                        )
+                    ]
+
+                    def landed(arrive=arrive, relay=relay, pair_of=pair_of):
+                        arrive[0].receive()
+                        relay.start()
+                        pair_of[0].start_own()
+
+                    def relayed(relay=relay, pair_of=pair_of):
+                        relay.receive()
+                        pair_of[1].start_own()
+
+                    steps = (landed, pair_of[0].forward, relayed, pair_of[1].forward)
+                    relays.append(relay)
+                else:
+                    pair_of = [
+                        Spread(size, place, lambda held, cut=cut: arrivals.at[held, :, cut], part_send,
+                               part_recv, base)
+                    ]
+
+                    def landed(arrive=arrive, pair_of=pair_of):
+                        for move in arrive:
+                            move.receive()
+                        pair_of[0].start_own()
+
+                    steps = (landed, pair_of[0].forward)
+                part_spreads += pair_of
+                actions += list(zip(PLAN[min(level, 2) - 1][c % 4], steps))
+            actions.sort(key=lambda item: item[0])
 
             def beside(j, late):
-                if late:
-                    pl.when(j == 0)(pending)
-                for c in range(size):
-                    land_at, pass_at = PLAN[min(level, 2) - 1][c % 4]
-                    if land_at % 2 == late:
-
-                        @pl.when(j == land_at // 2)
-                        def _():
-                            for move in part_moves[c]:
-                                move.receive()
-                            part_spreads[c].start_own()
-
-                    if pass_at % 2 == late:
-                        pl.when(j == pass_at // 2)(part_spreads[c].forward)
+                for point, act in actions:
+                    if point % 2 == late and point < 2 * size:
+                        pl.when(j == point // 2)(act)
 
             factor(work, high, low, beside)
-            for c in range(size):
-                if PLAN[min(level, 2) - 1][c % 4][1] >= 2 * size:
-                    part_spreads[c].forward()
+            for point, act in actions:
+                if point >= 2 * size:
+                    act()
             for one in part_spreads:
                 one.finish()
-            sending += part_spreads
+            sending += part_spreads + relays
             for b in range(size):
                 for part in range(2):
                     top, bottom = split(arrivals[b, part])
@@ -491,7 +530,8 @@
         lower = None if level == 0 else right_low
         term_moves, turned = [None, None], [None, None]
         for part in (1, 0) if last else (0, 1):
-            solve(high, low, right_high, lower, solved_high, solved_low, part, size)
+            turn = part == 1 and level < 2
+            solve(high, low, right_high, lower, solved_high, solved_low, part, size, turn)
             pair = lambda b, part=part: (solved_high[:, column(part, b)], solved_low[:, column(part, b)])
             own = pair(place)
             own = (own[0].T, own[1].T)
@@ -520,22 +560,33 @@
                     (level * 2 + part) * len(share_cuts) + d,
                     me + distance if part == 0 else me - distance, sends, receives,
                 )
-                move.start()
                 moves.append(move)
+            moves[0].start()
+            if last:
+                for move in moves[1:]:
+                    move.start()
             term_moves[part] = moves
+
+        if not last:
+            for d in range(1, len(share_cuts)):
+                for part in range(2):
+                    term_moves[part][d].start()
 
         cross_moves = []
         if not last:
             cross[level, 0] = joined(turned[1], whole(0), (1, 0))
-            cross[level, 1] = joined(turned[0], whole(1), (1, 0))
+            if level > 0:
+                cross[level, 1] = joined(turned[0], whole(1), (1, 0))
             target = parts.at[level]
             for c in range(size):
-                cut = pl.ds(c * piece, piece)
+                cut = bands[level][c]
                 index = (level * size + c) * 2
                 cross_moves.append(
                     Move(cross.at[level, 0, cut], target.at[place, 0, cut], cross_send, cross_recv,
                          index, me - distance, goes_down, comes_down)
                 )
+                if level == 0:
+                    continue
                 cross_moves.append(
                     Move(cross.at[level, 1, cut], target.at[place, 1, cut], cross_send, cross_recv,
                          index + 1, me + distance, behind & ahead, me >= 2 * distance)
@@ -694,6 +745,8 @@
         + dma((LEVELS - 1) * size * 2)
         + dma((LEVELS - 1) * kinds * hops)
         + dma((LEVELS - 1) * size * hops)
+        + dma(size)
+        + dma(size * hops)
         + dma(kinds),
         compiler_params=pltpu.CompilerParams(collective_id=0, has_side_effects=True),
     )(design[0], process[0], prior_prec, routes, counts)

time: 124 us -> 121 us (0.976)
  Pallas kernels: 121 us -> 118 us
    pallas_call x1, Pallas kernels: 121 us -> 118 us  [shards(): pl.pallas_call(functools.partial(kernel, times, size, total_slots, block_...]
where the time goes in v4:
time: 121 us
  Pallas kernels  118 us (98%)
  other arithmetic  1.96 us (2%)
  between operations  1.29 us (1%)
    pallas_call x1, Pallas kernels, shards(): pl.pallas_call(functools.partial(kernel, times, size, total_slots, block_...  118 us

profile of v4, /device:TPU:0, one launch (start us, length us, event | category | flops | bytes accessed | tf_op | source)
XLA Modules:
  0.0 120.8 jit_solution(1032163962968802263)
XLA Ops:
  1.3 117.5 %shard_map.68 = (f32[128,512]{1,0:T(8,128)}, f32[128,512]{1,0:T(8,128)}, f32[128,512]{1,0:T(8,128)}) custom-call(bf16[512,512]{1,0:T(8,128)(2,1)} %bitcast.6, bf16[128,512]{1,0:T(8,128)(2,1)} %bitcast.7, f32[1,128]{1,0:T(1,128)} %prior_ref.1, s32[1,4]{1,0:T(1,128)} %routes_ref.1, s32[1,1]{1,0:T(1,128)S(6)} %copy.7.counts_ref), custom_call_target="tpu_custom_call" | custom-call | tf_op jit(solution)/shard_map/pallas_call | solution.py:713
  118.8 2.0 %negate_bitcast_fusion = (f32[1,128,512]{2,1,0:T(8,128)}, f32[1,128,512]{2,1,0:T(8,128)}) fusion(f32[128,512]{1,0:T(8,128)} %get-tuple-element.7, f32[128,512]{1,0:T(8,128)} %get-tuple-element.5, f32[128,512]{1,0:T(8,128)} %get-tuple-element.6), kind=kLoop, calls=%fused_computation | loop fusion | flops 131072 | bytes 1310720 | tf_op jit(solution)/shard_map/neg | solution.py:753

commit v5 on v4

--- a/solution.py
+++ b/solution.py
@@ -10,9 +10,10 @@
 LEVELS = 3
 W = 8
 SHARES = ((5, 5, 4, 2), (3, 5, 4, 4))
+POINTS = 5
 PLAN = (
-    ((1, 3, 3, 6), (2, 4, 4, 7), (3, 5, 5, 8), (3, 5, 6, 8)),
-    ((0, 3), (1, 5), (2, 6), (3, 7)),
+    ((2, 7, 7, 15), (4, 9, 9, 17), (7, 12, 12, 19), (7, 13, 13, 20)),
+    ((0, 6), (0, 11), (2, 14), (4, 18)),
 )
 MESH = pl.DeviceIdType.MESH
 
@@ -58,7 +59,7 @@
             values[k] = values[k] - lower[k, s] * out[s]
     return out
 
-def factor_inverse(m, panel=32):
+def factor_inverse(m, panel=32, between=None):
     n = m.shape[0]
     rows = [m[W * g : W * (g + 1), :] for g in range(n // W)]
     lane = lax.broadcasted_iota(jnp.int32, (W, n), 1)
@@ -112,6 +113,8 @@
                 two = forward(two, scale2, lower2)
                 rows[i] = take(take(rows[i], one, solved, first), two, solved2, second)
         if end < n // W:
+            if between is not None:
+                between(p + 1)
             edge = end * W
             kept = lambda g: jnp.where((lane < (g + 1) * W) | (lane >= edge), rows[g], 0.0)
             done = jnp.concatenate([kept(g) for g in range(p * per, end)], axis=0)
@@ -143,22 +146,25 @@
         at = pl.ds(pl.multiple_of(j * rows, rows), rows)
         if beside is not None:
             beside(j, 0)
-        inverse = factor_inverse(work[j, :, at])
+        between = None if beside is None else functools.partial(beside, j)
+        inverse = factor_inverse(work[j, :, at], between=between)
         if beside is not None:
-            beside(j, 1)
+            beside(j, POINTS - 1)
         work[j, :, at] = unit
         solved = joined(split(inverse), split(work[j]), (1, 0))
         solved_high, solved_low = split(solved)
         high[at, :] = solved_high
         low[at, :] = solved_low
-        for i in range(1, blocks):
-
-            @pl.when(i > j)
+        for done in range(blocks - 1):
+
+            @pl.when(j == done)
             def _():
-                cut = slice(i * rows, (i + 1) * rows)
-                left = (high[at, cut].T, low[at, cut].T)
-                work[i, :, at] = jnp.zeros((rows, rows), jnp.float32)
-                work[i] = work[i] - joined(left, (solved_high, solved_low), (1, 0))
+                here = slice(done * rows, (done + 1) * rows)
+                for i in range(done + 1, blocks):
+                    cut = slice(i * rows, (i + 1) * rows)
+                    left = (high[here, cut].T, low[here, cut].T)
+                    work[i, :, here] = jnp.zeros((rows, rows), jnp.float32)
+                    work[i] = work[i] - joined(left, (solved_high, solved_low), (1, 0))
 
         keep = column_block <= j
         high[at, :] = jnp.where(keep, solved_high, 0.0).astype(jnp.bfloat16)
@@ -452,7 +458,7 @@
             has_next = me + 2 * below <= times
             has_previous = me >= 2 * below
 
-            part_spreads, relays, actions = [], [], [(1, pending)]
+            part_spreads, relays, actions = [], [], [(POINTS - 1, pending)]
             for c in range(size):
                 cut = bands[level - 1][c]
                 base = ((level - 1) * size + c) * hops
@@ -503,14 +509,14 @@
                 actions += list(zip(PLAN[min(level, 2) - 1][c % 4], steps))
             actions.sort(key=lambda item: item[0])
 
-            def beside(j, late):
+            def beside(j, spot):
                 for point, act in actions:
-                    if point % 2 == late and point < 2 * size:
-                        pl.when(j == point // 2)(act)
+                    if point % POINTS == spot and point < POINTS * size:
+                        pl.when(j == point // POINTS)(act)
 
             factor(work, high, low, beside)
             for point, act in actions:
-                if point >= 2 * size:
+                if point >= POINTS * size:
                     act()
             for one in part_spreads:
                 one.finish()

time: 121 us -> 119 us (0.983)
  Pallas kernels: 118 us -> 116 us
    pallas_call x1, Pallas kernels: 118 us -> 116 us  [shards(): pl.pallas_call(functools.partial(kernel, times, size, total_slots, block_...]
where the time goes in v5:
time: 119 us
  Pallas kernels  116 us (97%)
  other arithmetic  1.96 us (2%)
  between operations  1.29 us (1%)
    pallas_call x1, Pallas kernels, shards(): pl.pallas_call(functools.partial(kernel, times, size, total_slots, block_...  116 us

profile of v5, /device:TPU:0, one launch (start us, length us, event | category | flops | bytes accessed | tf_op | source)
XLA Modules:
  0.0 118.9 jit_solution(3325102728552207210)
XLA Ops:
  1.3 115.7 %shard_map.68 = (f32[128,512]{1,0:T(8,128)}, f32[128,512]{1,0:T(8,128)}, f32[128,512]{1,0:T(8,128)}) custom-call(bf16[512,512]{1,0:T(8,128)(2,1)} %bitcast.6, bf16[128,512]{1,0:T(8,128)(2,1)} %bitcast.7, f32[1,128]{1,0:T(1,128)} %prior_ref.1, s32[1,4]{1,0:T(1,128)} %routes_ref.1, s32[1,1]{1,0:T(1,128)S(6)} %copy.7.counts_ref), custom_call_target="tpu_custom_call" | custom-call | tf_op jit(solution)/shard_map/pallas_call | solution.py:719
  117.0 2.0 %negate_bitcast_fusion = (f32[1,128,512]{2,1,0:T(8,128)}, f32[1,128,512]{2,1,0:T(8,128)}) fusion(f32[128,512]{1,0:T(8,128)} %get-tuple-element.7, f32[128,512]{1,0:T(8,128)} %get-tuple-element.5, f32[128,512]{1,0:T(8,128)} %get-tuple-element.6), kind=kLoop, calls=%fused_computation | loop fusion | flops 131072 | bytes 1310720 | tf_op jit(solution)/shard_map/neg | solution.py:759
